TPU v7x, 512 devices: a whole 4x4x16 slice. The times are simulated.
512 devices in a mesh: seq: 64 (over y, z), head: 8 (over x, core).
Axes of the slice: x: 4, y: 4, z: 16, core: 2. Of those that a mesh axis runs over, the one named last changes fastest.
Arguments:
- queries: bfloat16 [16384, 8192], P(('seq', 'head')), may hold values from -6 to 6
- keys: bfloat16 [16384, 8192], P(('seq', 'head')), may hold values from -6 to 6
- values: bfloat16 [16384, 8192], P(('seq', 'head')), may hold values from -70 to 70
- log_decay: float32 [64, 16384], P('head', 'seq'), may hold values from -1 to 0
- doc_lengths: int32 [32], replicated, may hold values from 1 to 4096, 16384 in all
- gain: float32 [8192], P('head'), may hold values from 0.25 to 1.75
Outputs:
- attended: bfloat16 [16384, 8192], P(('seq', 'head'))
All inputs are finite; a program needn't handle non-finite values.
Results may differ from a plain program's by a relative error of at most 0.001.
Values may be sent and summed in bfloat16 or wider, within the bound.
No kernel may reach another device: no remote copies, remote signals or barrier semaphores. Data moves between devices by JAX's collectives and lax.ppermute only.
A program may use at most 128 MiB of HBM per device.

v0:
```python
import jax
import jax.numpy as jnp
from jax import lax
from jax.sharding import PartitionSpec as P

HIGHEST = lax.Precision.HIGHEST


def prefix(part, axis, combine, identity):
    place = lax.axis_index(axis)
    gathered = jax.tree.map(lambda a: lax.all_gather(a, axis), part)
    state = jax.tree.map(lambda a, e: jnp.zeros_like(a) + jnp.asarray(e, a.dtype), part, identity)

    def one(turn, state):
        return combine(
            state, jax.tree.map(lambda a: lax.dynamic_index_in_dim(a, turn, 0, False), gathered)
        )

    return lax.fori_loop(0, place, one, state)


def link(earlier, later):
    factor_one, state_one = earlier
    factor_two, state_two = later
    return (factor_one * factor_two, factor_two[:, None, None] * state_one + state_two)


def make_identity(amount, head_width):
    return (
        jnp.ones((amount,), jnp.float32),
        jnp.zeros((amount, head_width, head_width), jnp.float32),
    )


def local(queries, keys, values, log_decay, doc_lengths, gain):
    query_rows, key_rows, value_rows = (
        lax.all_to_all(queries, "head", split_axis=1, concat_axis=0, tiled=True),
        lax.all_to_all(keys, "head", split_axis=1, concat_axis=0, tiled=True),
        lax.all_to_all(values, "head", split_axis=1, concat_axis=0, tiled=True),
    )
    head_count = log_decay.shape[0]
    row_count = key_rows.shape[0]
    head_width = key_rows.shape[1] // head_count
    doc_ends = jnp.cumsum(doc_lengths)
    first_row = lax.axis_index("seq") * row_count
    positions = first_row + jnp.arange(row_count, dtype=jnp.int32)
    doc_ids = jnp.sum((doc_ends[None, :] <= positions[:, None]).astype(jnp.int32), axis=1)
    prior_doc = jnp.sum((doc_ends <= first_row - 1).astype(jnp.int32))
    order_ids = jnp.arange(row_count, dtype=jnp.int32)
    allowed = (order_ids[:, None] >= order_ids[None, :]) & (doc_ids[:, None] == doc_ids[None, :])
    decay_sum = jnp.cumsum(log_decay, axis=1)
    tailing = (
        jnp.exp(decay_sum[:, -1:] - decay_sum)
        * (doc_ids == doc_ids[-1]).astype(jnp.float32)[None, :]
    )
    leading = jnp.exp(decay_sum) * (doc_ids == prior_doc).astype(jnp.float32)[None, :]
    carried = jnp.exp(decay_sum[:, -1]) * (doc_ids[-1] == prior_doc).astype(jnp.float32)
    head_ids = jnp.arange(head_count, dtype=jnp.int32)

    def pick(block, head_index):
        return lax.dynamic_slice_in_dim(block, head_index * head_width, head_width, 1)

    def own_state(head_index):
        weighted = pick(key_rows, head_index).astype(jnp.float32) * tailing[head_index][:, None]
        value_part = pick(value_rows, head_index).astype(jnp.float32)
        return jnp.einsum(
            "jd,je->de", weighted, value_part, precision=HIGHEST, preferred_element_type=jnp.float32
        )

    def within(head_index):
        scores = lax.dot_general(
            pick(query_rows, head_index),
            pick(key_rows, head_index),
            (((1,), (1,)), ((), ())),
            preferred_element_type=jnp.float32,
        )
        gaps = decay_sum[head_index][:, None] - decay_sum[head_index][None, :]
        weights = jnp.where(allowed, jnp.exp(jnp.where(allowed, gaps, 0.0)), 0.0)
        value_part = pick(value_rows, head_index).astype(jnp.float32)
        return jnp.dot(
            scores * weights, value_part, precision=HIGHEST, preferred_element_type=jnp.float32
        )

    def across(paired):
        head_index, state = paired
        scaled = pick(query_rows, head_index).astype(jnp.float32) * leading[head_index][:, None]
        return jnp.dot(scaled, state, precision=HIGHEST, preferred_element_type=jnp.float32)

    own = lax.map(own_state, head_ids)
    total_factor, incoming = prefix(
        (carried, own), "seq", link, make_identity(head_count, head_width)
    )
    far = lax.map(across, (head_ids, incoming))
    near = lax.map(within, head_ids)
    mixed = near + far
    mean_square = jnp.mean(mixed * mixed, axis=-1, keepdims=True)
    normed = mixed * lax.rsqrt(mean_square + 1e-06) * gain.reshape(head_count, 1, head_width)
    merged = (
        jnp.transpose(normed, (1, 0, 2))
        .reshape(row_count, head_count * head_width)
        .astype(jnp.bfloat16)
    )
    return lax.all_to_all(merged, "head", split_axis=0, concat_axis=1, tiled=True)


def solution(mesh):
    return jax.shard_map(
        local,
        mesh=mesh,
        in_specs=(
            P(("seq", "head"), None),
            P(("seq", "head"), None),
            P(("seq", "head"), None),
            P("head", "seq"),
            P(),
            P("head"),
        ),
        out_specs=P(("seq", "head"), None),
        check_vma=False,
    )
```

profile of v0, /device:TPU:504, one launch (start us, length us, event | category | flops | bytes accessed | tf_op | source)
XLA Modules:
  0.0 483.5 jit_solution(14517840087160387409)
XLA Ops:
  6.5 1.9 copy.42
  8.4 4.3 all-to-all-start.1
  14.3 1.2 reduce-window.18
  17.7 1.9 copy.41
  19.5 1.2 compare_convert_fusion
  20.7 2.3 all-to-all-done.1
  23.1 3.5 all-to-all-start.2
  27.0 9.9 %all-to-all-done.2 = bf16[32,8,1024]{2,0,1:T(8,128)(2,1)S(1)} async-done(((bf16[32,8,1024]{2,0,1:T(8,128)(2,1)}), bf16[32,8,1024]{2,0,1:T(8,128)(2,1)S(1)}, u32[]{:S(2)}, u32[]{:S(2)}) %all-to-all-start.2) | async-done | bytes 524320 | tf_op jit(solution)/shard_map/all_to_all | solution.py:39
  36.9 28.6 %while.43 = (s32[]{:T(128)}, f32[8,128,128]{2,1,0:T(8,128)S(1)}, s32[8]{0:T(128)S(1)}, bf16[256,1024]{1,0:T(8,128)(2,1)S(1)}, f32[8,256]{1,0:T(8,128)S(1)}, /*in...) while((s32[]{:T(128)}, f32[8,128,128]{2,1,0:T(8,128)S(1)}, ...), condition=%wide.region_8.9_spmd, body=%wide.region_7.8_spmd.sunk | while | flops 50397192 | bytes 200913 | solution.py:89
  66.3 1.9 copy.43
  68.2 3.5 all-to-all-start
  71.7 1.3 dynamic-slice
  73.9 139.0 %all-reduce = f32[512]{0:T(512)S(1)} all-reduce(f32[512]{0:T(512)S(1)} %dynamic-update-slice), channel_id=2, replica_groups=mesh['seq'=64,'head'=8] {'seq'}, use_global_device_ids=true, to_apply=%add | all-reduce | flops 512 | bytes 4096
  213.1 29.7 %while.46 = (s32[]{:T(128)}, f32[8,256,128]{2,1,0:T(8,128)S(1)}, s32[8]{0:T(128)S(1)}, bf16[256,1024]{1,0:T(8,128)(2,1)S(1)}, bf16[256,1024]{1,0:T(8,128)(2,1)S(...) while((s32[]{:T(128)}, f32[8,256,128]{2,1,0:T(8,128)S(1)}, ...), condition=%wide.region_5.6_spmd.clone, body=%wide.region_4.5_spmd.clone.sunk | while | flops 117899272 | bytes 859365 | solution.py:94
  242.8 110.3 %all-gather.4.cloned.1.call-done = f32[512,128,128]{2,1,0:T(8,128)} async-done(((f32[8,128,128]{2,1,0:T(8,128)}), f32[512,128,128]{2,1,0:T(8,128)}) %all-gather.4.cloned.1.call-update) | async-done | bytes 33554448 | tf_op jit(solution)/shard_map/all_gather | solution.py:11
  353.1 77.9 %while.44 = (s32[]{:T(128)}, f32[8,128,128]{2,1,0:T(8,128)S(1)}, s32[]{:T(128)}, f32[64,8]{1,0:T(8,128)S(1)}, f32[64,8,128,128]{3,2,1,0:T(8,128)}, /*index=5*/s32[]{:T(128)}, s32[]{:T(128)}, s32[]{:T(128)}) while((s32[]{:T(128)}, f32[8,128,128]{2,1,0:T(8,128)S(1)}, s32[]{:T(128)}, f32[64,8]{1,0:T(8,128)S(1)}, ...), condition=%wide.region_10.11_spmd, body=%wide.region_9.10_spmd.sunk | while | flops 262149 | bytes 1573087 | solution.py:19
  353.2 1.2 bitcast_add_fusion.2
  354.4 1.2 bitcast_add_fusion.2
  355.6 1.2 bitcast_add_fusion.2
  356.9 1.2 bitcast_add_fusion.2
  358.1 1.2 bitcast_add_fusion.2
  359.4 1.2 bitcast_add_fusion.2
  360.6 1.2 bitcast_add_fusion.2
  361.8 1.2 bitcast_add_fusion.2
  363.1 1.2 bitcast_add_fusion.2
  364.3 1.2 bitcast_add_fusion.2
  365.5 1.2 bitcast_add_fusion.2
  366.8 1.2 bitcast_add_fusion.2
  368.0 1.2 bitcast_add_fusion.2
  369.2 1.2 bitcast_add_fusion.2
  370.5 1.2 bitcast_add_fusion.2
  371.7 1.2 bitcast_add_fusion.2
  372.9 1.2 bitcast_add_fusion.2
  374.2 1.2 bitcast_add_fusion.2
  375.4 1.2 bitcast_add_fusion.2
  376.7 1.2 bitcast_add_fusion.2
  377.9 1.2 bitcast_add_fusion.2
  379.1 1.2 bitcast_add_fusion.2
  380.4 1.2 bitcast_add_fusion.2
  381.6 1.2 bitcast_add_fusion.2
  382.8 1.2 bitcast_add_fusion.2
  384.1 1.2 bitcast_add_fusion.2
  385.3 1.2 bitcast_add_fusion.2
  386.5 1.2 bitcast_add_fusion.2
  387.8 1.2 bitcast_add_fusion.2
  389.0 1.2 bitcast_add_fusion.2
  390.2 1.2 bitcast_add_fusion.2
  391.5 1.2 bitcast_add_fusion.2
  392.7 1.2 bitcast_add_fusion.2
  394.0 1.2 bitcast_add_fusion.2
  395.2 1.2 bitcast_add_fusion.2
  396.4 1.2 bitcast_add_fusion.2
  397.7 1.2 bitcast_add_fusion.2
  400.1 1.2 bitcast_add_fusion.2
  402.6 1.2 bitcast_add_fusion.2
  405.1 1.2 bitcast_add_fusion.2
  407.6 1.2 bitcast_add_fusion.2
  410.0 1.2 bitcast_add_fusion.2
  421.1 1.2 bitcast_add_fusion.2
  423.6 1.2 bitcast_add_fusion.2
  426.1 1.2 bitcast_add_fusion.2
  428.6 1.2 bitcast_add_fusion.2
  431.1 28.3 %while.45 = (s32[]{:T(128)}, f32[8,256,128]{2,1,0:T(8,128)S(1)}, s32[8]{0:T(128)S(1)}, bf16[256,1024]{1,0:T(8,128)(2,1)S(1)}, f32[8,256]{1,0:T(8,128)S(1)}, /*in...) while((s32[]{:T(128)}, f32[8,256,128]{2,1,0:T(8,128)S(1)}, ...), condition=%wide.region_12.13_spmd, body=%wide.region_11.12_spmd.sunk | while | flops 50397192 | bytes 266449 | solution.py:93
  461.4 14.4 %all_to_all.73 = bf16[8,32,1024]{2,1,0:T(8,128)(2,1)S(1)} all-to-all(bf16[8,32,1024]{2,1,0:T(8,128)(2,1)S(1)} %convert_element_type.48), channel_id=1, replica_groups=mesh['seq'=64,'head'=8] {'head'}, dimensions={0} | all-to-all | bytes 1048576 | tf_op jit(solution)/shard_map/all_to_all | solution.py:103
  (194 shorter events, 51.5 us)
Async XLA Ops:
  8.4 14.6 %all-to-all-start.1 = ((bf16[32,8,1024]{2,0,1:T(8,128)(2,1)}), bf16[32,8,1024]{2,0,1:T(8,128)(2,1)S(1)}, u32[]{:S(2)}, u32[]{:S(2)}) async-start(bf16[32,8,1024]{2,0,1:T(8,128)(2,1)} %bitcast.59), calls=%async_computation.1 | async-start | bytes 1048576 | tf_op jit(solution)/shard_map/all_to_all | solution.py:38
  23.1 13.8 %all-to-all-start.2 = ((bf16[32,8,1024]{2,0,1:T(8,128)(2,1)}), bf16[32,8,1024]{2,0,1:T(8,128)(2,1)S(1)}, u32[]{:S(2)}, u32[]{:S(2)}) async-start(bf16[32,8,1024]{2,0,1:T(8,128)(2,1)} %bitcast.58), calls=%async_computation.2 | async-start | bytes 1048576 | tf_op jit(solution)/shard_map/all_to_all | solution.py:39
  26.6 326.5 %all-gather.4.cloned.1.call-start = ((), (), s32[]{:S(2)}) async-start(), calls=%async_computation.4 | async-start | bytes 34078720 | tf_op jit(solution)/shard_map/all_gather | solution.py:11
  65.5 0.8 copy-start
  68.2 144.8 %all-to-all-start = ((bf16[32,8,1024]{2,0,1:T(8,128)(2,1)}), bf16[32,8,1024]{2,0,1:T(8,128)(2,1)S(1)}, u32[]{:S(2)}, u32[]{:S(2)}) async-start(bf16[32,8,1024]{2,0,1:T(8,128)(2,1)} %bitcast.60), calls=%async_computation | async-start | bytes 1048576 | tf_op jit(solution)/shard_map/all_to_all | solution.py:37
Sparse Core Ops, SparseCore 0:
  66.4 286.6 all-gather.3
where the time goes:
time: 488 us; the launch traced here: 484 us
  blocking collectives  153 us (31%)
  waiting for transfers between devices  122 us (25%)
  other arithmetic  80.2 us (16%)
  loops' own time  65.2 us (13%)
  local copies, waits for them, and re-layouts  26.1 us (5%)
  between operations  15.4 us (3%)
  starting transfers between devices  11.3 us (2%)
  matrix products  9.34 us (2%)
    unnamed x1, blocking collectives  139 us
    all_gather x1, waiting for transfers between devices, prefix(): gathered = jax.tree.map(lambda a: lax.all_gather(a, axis), part)  110 us
    add x63, other arithmetic, link(): factor_two[:, None, None] * state_one + state_two  75 us
    another operation x1, loops' own time, local(): near = lax.map(within, head_ids)  21.1 us
    another operation x1, loops' own time, local(): far = lax.map(across, (head_ids, incoming))  21 us
    another operation x1, loops' own time, local(): own = lax.map(own_state, head_ids)  21 us
    all_to_all x1, blocking collectives, local(): lax.all_to_all(merged, 'head', split_axis=0, concat_axis=1, tiled=True)  14.4 us
    dynamic_slice x24, local copies, waits for them, and re-layouts, local(): own = lax.map(own_state, head_ids)  14.1 us
  transfers between devices with their start and end apart: 4, of which 3 were waited for; matrix products, arithmetic and copies ran while one was open for 4% of the time, Pallas kernels for 0%

commit v1 on v0

v1 whole, which is shorter than its diff:
```python
import functools

import jax
import jax.numpy as jnp
from jax import lax
from jax.experimental import pallas as pl
from jax.experimental.pallas import tpu as pltpu
from jax.sharding import PartitionSpec as P

F32 = jnp.float32
BF16 = jnp.bfloat16
DH = 128
CH = 128
NC = 4
PAIR = 2
NH = 4
SEG = CH * NC
GROUP = 16
ROWS = 16
VMEM_LIMIT = 48 * 1024 * 1024


def split2(x):
    high = x.astype(BF16)
    return high, (x - high.astype(F32)).astype(BF16)


def split3(x):
    high = x.astype(BF16)
    rest = x - high.astype(F32)
    mid = rest.astype(BF16)
    return high, mid, (rest - mid.astype(F32)).astype(BF16)


def dot(a, b):
    return jnp.dot(a, b, preferred_element_type=F32)


def pack_kernel(q_ref, k_ref, v_ref, out_ref, sems):
    copies = []
    for place in range(GROUP):
        column = (2 * (place % 8) + place // 8) * NH * DH
        for which, ref in enumerate((q_ref, k_ref, v_ref)):
            copies.append(
                pltpu.make_async_copy(
                    ref.at[:, pl.ds(column, NH * DH)],
                    out_ref.at[place, which],
                    sems.at[place, which],
                )
            )
    for copy in copies:
        copy.start()
    for copy in copies:
        copy.wait()


def unpack_kernel(in_ref, out_ref, sems):
    copies = []
    for place in range(GROUP):
        column = (2 * (place % 8) + place // 8) * NH * DH
        copies.append(
            pltpu.make_async_copy(
                in_ref.at[place], out_ref.at[:, pl.ds(column, NH * DH)], sems.at[place]
            )
        )
    for copy in copies:
        copy.start()
    for copy in copies:
        copy.wait()


def pick_heads(tile, half):
    return jnp.where(half == 0, tile, pltpu.roll(tile, 4, axis=0))


def state_kernel(place_ref, lengths_ref, own_ref, other_ref, k_ref, v_ref, send_ref, rows_ref, cols_ref):
    segment, half = place_ref[0], place_ref[1]
    own, other = own_ref[...], other_ref[...]
    first = jnp.where(half == 0, own, other)
    second = jnp.where(half == 0, other, own)
    decay = jnp.concatenate(
        [
            pick_heads(part[:, i * CH : (i + 1) * CH], half)
            for part in (first, second)
            for i in range(2)
        ],
        axis=0,
    )
    upper = (
        lax.broadcasted_iota(jnp.int32, (CH, CH), 0) <= lax.broadcasted_iota(jnp.int32, (CH, CH), 1)
    ).astype(BF16)
    high, mid, low = split3(decay)
    sums = dot(high, upper) + (dot(mid, upper) + dot(low, upper))

    lane = lax.broadcasted_iota(jnp.int32, (8, CH), 1)
    start = segment * SEG
    spots = [jnp.full((8, CH), start - 1, jnp.int32)] + [start + c * CH + lane for c in range(NC)]
    ids = [jnp.zeros((8, CH), jnp.int32) for _ in spots]
    end = jnp.int32(0)
    for d in range(lengths_ref.shape[0]):
        end = end + lengths_ref[d]
        ids = [i + (end <= s).astype(jnp.int32) for i, s in zip(ids, spots)]

    def last(tile):
        return jnp.broadcast_to(tile[:, CH - 1 : CH], (8, CH))

    prior = ids[0]
    tails, leads, carries = [], [], []
    for c in range(NC):
        local, here = sums[8 * c : 8 * c + 8], ids[c + 1]
        total, closing = last(local), last(here)
        tails.append(jnp.where(here == closing, jnp.exp(total - local), 0.0))
        leads.append(jnp.where(here == prior, jnp.exp(local), 0.0))
        carries.append(jnp.where(closing == prior, jnp.exp(total), 0.0))
        prior = closing
    before = [jnp.ones((8, CH), F32)]
    for c in range(NC):
        before.append(before[-1] * carries[c])
    after = [jnp.ones((8, CH), F32)]
    for c in range(NC - 1, 0, -1):
        after.append(after[-1] * carries[c])
    after = after[::-1]
    rows_ref[0:32] = sums
    rows_ref[32:64] = jnp.concatenate(tails, axis=0)
    rows_ref[64:96] = jnp.concatenate(carries, axis=0)
    rows_ref[96:128] = jnp.concatenate([i.astype(F32) for i in ids[1:]], axis=0)
    table = jnp.concatenate(
        [sums]
        + leads
        + [lead * b for lead, b in zip(leads, before)]
        + [i.astype(F32) for i in ids[1:]],
        axis=0,
    )
    cols_ref[...] = table.T

    full_tails = [t * a for t, a in zip(tails, after)]
    for head in range(NH):
        at = slice(head * DH, (head + 1) * DH)
        key_part = k_ref[:, 0, :, at].reshape(SEG, DH)
        value_part = v_ref[:, 0, :, at].reshape(SEG, DH)
        weight = jnp.concatenate([t[head : head + 1] for t in full_tails], axis=1)
        weighted = key_part.T.astype(F32) * weight
        both = dot(jnp.concatenate(split2(weighted), axis=0), value_part)
        state = both[:DH] + both[DH:]
        factor = jnp.broadcast_to(before[NC][head : head + 1], (8, DH))
        for piece in range(DH // ROWS):
            send_ref[head * (DH // ROWS) + piece, :ROWS] = state[piece * ROWS : (piece + 1) * ROWS]
            send_ref[head * (DH // ROWS) + piece, ROWS:] = factor


def near_kernel(q_ref, k_ref, v_ref, rows_ref, cols_ref, near_ref):
    order = lax.broadcasted_iota(jnp.int32, (CH, CH), 0) >= lax.broadcasted_iota(
        jnp.int32, (CH, CH), 1
    )
    cols = cols_ref[...]
    masks = []
    for c in range(NC):
        ids_row = rows_ref[96 + 8 * c : 97 + 8 * c]
        ids_col = cols[:, 96 + 8 * c : 97 + 8 * c]
        masks.append(order & (ids_col == ids_row))
    for head in range(NH):
        at = slice(head * DH, (head + 1) * DH)
        state = None
        for c in range(NC):
            part = slice(4 * c, 4 * c + 4)
            row = 8 * c + head
            query = q_ref[part, 0, :, at].reshape(CH, DH)
            key_part = k_ref[part, 0, :, at].reshape(CH, DH)
            value_part = v_ref[part, 0, :, at].reshape(CH, DH)
            keys_across = key_part.T
            gaps = cols[:, row : row + 1] - rows_ref[row : row + 1]
            weights = jnp.where(masks[c], jnp.exp(jnp.where(masks[c], gaps, 0.0)), 0.0)
            high, low = split2(dot(query, keys_across) * weights)
            mixed = dot(high, value_part) + dot(low, value_part)
            if c:
                both = dot(query, jnp.concatenate(split2(state), axis=1))
                mixed = mixed + (both[:, :DH] + both[:, DH:]) * cols[:, 32 + row : 33 + row]
            near_ref[head, c * CH : (c + 1) * CH] = mixed
            if c < NC - 1:
                weighted = keys_across.astype(F32) * rows_ref[32 + row : 33 + row]
                both = dot(jnp.concatenate(split2(weighted), axis=0), value_part)
                own = both[:DH] + both[DH:]
                state = own if c == 0 else own + state * rows_ref[64 + row : 65 + row]


def scan_kernel(in_ref, out_ref):
    state = jnp.zeros((ROWS, DH), F32)
    for segment in range(in_ref.shape[0]):
        out_ref[segment] = state
        factor = in_ref[segment, ROWS : ROWS + 1]
        state = state * factor + in_ref[segment, :ROWS]


def close_kernel(place_ref, q_ref, state_ref, near_ref, cols_ref, gain_ref, out_ref):
    gain = pick_heads(gain_ref[...], place_ref[1])
    cols = cols_ref[...]
    for head in range(NH):
        at = slice(head * DH, (head + 1) * DH)
        query = q_ref[:, 0, :, at].reshape(SEG, DH)
        both = dot(query, jnp.concatenate(split2(state_ref[head]), axis=1))
        far = both[:, :DH] + both[:, DH:]
        for c in range(NC):
            column = 64 + 8 * c + head
            mixed = near_ref[head, c * CH : (c + 1) * CH] + far[c * CH : (c + 1) * CH] * (
                cols[:, column : column + 1]
            )
            square = jnp.mean(mixed * mixed, axis=-1, keepdims=True)
            normed = mixed * lax.rsqrt(square + 1e-06) * gain[head : head + 1]
            out_ref[4 * c : 4 * c + 4, :, at] = normed.astype(BF16).reshape(4, CH // 4, DH)


VMEM = pl.BlockSpec(memory_space=pltpu.VMEM)
SMEM = pl.BlockSpec(memory_space=pltpu.SMEM)
ANY = pl.BlockSpec(memory_space=pl.ANY)
PARAMS = pltpu.CompilerParams(vmem_limit_bytes=VMEM_LIMIT)


def part_spec(which):
    return pl.BlockSpec((GROUP, 1, SEG // GROUP, NH * DH), lambda i: (0, which, 0, 0))


def whole(*shape):
    return pl.BlockSpec(shape, lambda i: (0,) * len(shape))


def shaped(shape, kind=F32):
    return jax.ShapeDtypeStruct(shape, kind)


def local(seq_size, head_size, queries, keys, values, log_decay, doc_lengths, gain):
    tokens = queries.shape[0]
    segments = seq_size // PAIR
    pieces = NH * DH // ROWS
    seq = lax.axis_index("seq")
    place = jnp.stack([seq // PAIR, seq % PAIR]).astype(jnp.int32)
    token_groups = [
        [g * GROUP + i for i in range(GROUP)] for g in range(seq_size * head_size // GROUP)
    ]
    scan_groups = [[g * PAIR + i for g in range(segments)] for i in range(PAIR)]

    other_decay = lax.ppermute(log_decay, "seq", [(s, s ^ 1) for s in range(seq_size)])
    sent = pl.pallas_call(
        pack_kernel,
        out_shape=shaped((GROUP, 3, tokens, NH * DH), BF16),
        in_specs=[ANY] * 3,
        out_specs=ANY,
        scratch_shapes=[pltpu.SemaphoreType.DMA((GROUP, 3))],
        name="pack",
    )(queries, keys, values)
    parts = lax.all_to_all(
        sent, ("seq", "head"), 0, 0, axis_index_groups=token_groups, tiled=True
    )
    own, rows, cols = pl.pallas_call(
        state_kernel,
        out_shape=(
            shaped((pieces, ROWS + 8, DH)),
            shaped((128, CH)),
            shaped((CH, 128)),
        ),
        grid=(1,),
        in_specs=[SMEM, SMEM, whole(8, SEG // PAIR), whole(8, SEG // PAIR), part_spec(1), part_spec(2)],
        out_specs=(whole(pieces, ROWS + 8, DH), whole(128, CH), whole(CH, 128)),
        compiler_params=PARAMS,
        name="state",
    )(place, doc_lengths, log_decay, other_decay, parts, parts)
    gathered = lax.all_to_all(own, "seq", 0, 0, axis_index_groups=scan_groups, tiled=True)
    near = pl.pallas_call(
        near_kernel,
        out_shape=shaped((NH, SEG, DH)),
        grid=(1,),
        in_specs=[part_spec(0), part_spec(1), part_spec(2), whole(128, CH), whole(CH, 128)],
        out_specs=whole(NH, SEG, DH),
        compiler_params=PARAMS,
        cost_estimate=pl.CostEstimate(flops=500000000, transcendentals=300000, bytes_accessed=4000000),
        name="near",
    )(parts, parts, parts, rows, cols)
    prefixes = pl.pallas_call(
        scan_kernel,
        out_shape=shaped((segments, ROWS, DH)),
        name="scan",
    )(gathered)
    incoming = lax.all_to_all(
        prefixes, "seq", 0, 0, axis_index_groups=scan_groups, tiled=True
    ).reshape(NH, DH, DH)
    normed = pl.pallas_call(
        close_kernel,
        out_shape=shaped((GROUP, tokens, NH * DH), BF16),
        grid=(1,),
        in_specs=[
            SMEM,
            part_spec(0),
            whole(NH, DH, DH),
            whole(NH, SEG, DH),
            whole(CH, 128),
            whole(8, DH),
        ],
        out_specs=whole(GROUP, tokens, NH * DH),
        compiler_params=PARAMS,
        name="close",
    )(place, parts, incoming, near, cols, gain.reshape(8, DH))
    returned = lax.all_to_all(
        normed, ("seq", "head"), 0, 0, axis_index_groups=token_groups, tiled=True
    )
    return pl.pallas_call(
        unpack_kernel,
        out_shape=shaped((tokens, GROUP * NH * DH), BF16),
        in_specs=[ANY],
        out_specs=ANY,
        scratch_shapes=[pltpu.SemaphoreType.DMA((GROUP,))],
        name="unpack",
    )(returned)


def solution(mesh):
    return jax.shard_map(
        functools.partial(local, mesh.shape["seq"], mesh.shape["head"]),
        mesh=mesh,
        in_specs=(
            P(("seq", "head"), None),
            P(("seq", "head"), None),
            P(("seq", "head"), None),
            P("head", "seq"),
            P(),
            P("head"),
        ),
        out_specs=P(("seq", "head"), None),
        check_vma=False,
    )
```

time: 488 us -> 186 us (0.38)
  the two profiles are of different devices: /device:TPU:504 before, /device:TPU:1 now
where the time goes in v1:
time: 186 us; the launch traced here: 185 us
  Pallas kernels  74.4 us (40%)
  blocking collectives  58.8 us (32%)
  waiting for transfers between devices  31.1 us (17%)
  starting transfers between devices  21 us (11%)
    pallas_call x1, Pallas kernels, local(): pl.pallas_call(pack_kernel, out_shape=shaped((GROUP, 3, tokens, NH * DH),...  49.2 us
    all_to_all x1, blocking collectives, local(): lax.all_to_all(own, 'seq', 0, 0, axis_index_groups=scan_groups, tiled=True)  39 us
    all_to_all x1, blocking collectives, local(): lax.all_to_all(normed, ('seq', 'head'), 0, 0, axis_index_groups=token_gro...  19.7 us
    pallas_call x1, Pallas kernels, local(): pl.pallas_call(unpack_kernel, out_shape=shaped((tokens, GROUP * NH * DH),...  17.1 us
    ppermute x1, waiting for transfers between devices, local(): lax.ppermute(log_decay, 'seq', [(s, s ^ 1) for s in range(seq_size)])  16 us
    all_to_all x1, waiting for transfers between devices, local(): lax.all_to_all(prefixes, 'seq', 0, 0, axis_index_groups=scan_groups, tile...  12.6 us
    all_to_all x1, starting transfers between devices, local(): lax.all_to_all(sent, ('seq', 'head'), 0, 0, axis_index_groups=token_group...  10.4 us
    all_to_all x1, starting transfers between devices, local(): lax.all_to_all(prefixes, 'seq', 0, 0, axis_index_groups=scan_groups, tile...  7.31 us
  transfers between devices with their start and end apart: 3, of which 3 were waited for; matrix products, arithmetic and copies ran while one was open for 0% of the time, Pallas kernels for 2%

profile of v1, /device:TPU:1, one launch (start us, length us, event | category | flops | bytes accessed | tf_op | source)
XLA Modules:
  0.0 185.4 jit_solution(3721171994391376800)
XLA Ops:
  0.0 49.2 %pack.1 = bf16[16,3,32,512]{3,2,1,0:T(8,128)(2,1)} custom-call(bf16[32,8192]{1,0:T(8,128)(2,1)} %q_ref.1, bf16[32,8192]{1,0:T(8,128)(2,1)} %k_ref.1, bf16[32,8192]{1,0:T(8,128)(2,1)} %v_ref.1), custom_call_target="tpu_custom_call" | custom-call | tf_op jit(solution)/shard_map/pack/pallas_call | solution.py:242
  49.2 0.0 copy-start
  49.2 0.0 copy-start.2
  49.2 10.4 %all-to-all-start = ((bf16[16,3,32,512]{3,2,1,0:T(8,128)(2,1)}), bf16[16,3,32,512]{3,2,1,0:T(8,128)(2,1)S(1)}, u32[]{:S(2)}, u32[]{:S(2)}) async-start(bf16[16,3,32,512]{3,2,1,0:T(8,128)(2,1)} %pack.1), calls=%async_computation | async-start | bytes 3145728 | tf_op jit(solution)/shard_map/all_to_all | solution.py:250
  59.6 0.0 copy-done
  59.6 3.3 %collective-permute-start = (f32[8,256]{1,0:T(8,128)S(1)}, f32[8,256]{1,0:T(8,128)S(1)}, u32[]{:S(2)}, u32[]{:S(2)}) collective-permute-start(f32[8,256]{1,0:T(8,128)S(1)} %copy-done), channel_id=1, source_target_pairs={{0,8},{8,0},{16,24},{24,16},{32,40},{40,32},{48,56},{56,48},{64,72... | collective-permute-start | bytes 24584 | tf_op jit(solution)/shard_map/ppermute | solution.py:241
  63.0 0.1 pad_add_fusion.place_ref
  63.0 16.0 %collective-permute-done.other_ref = f32[8,256]{1,0:T(8,128)S(1)} collective-permute-done((f32[8,256]{1,0:T(8,128)S(1)}, f32[8,256]{1,0:T(8,128)S(1)}, u32[]{:S(2)}, u32[]{:S(2)}) %collective-permute-start) | collective-permute-done | bytes 8224 | tf_op jit(solution)/shard_map/ppermute | solution.py:241
  79.0 2.5 %all-to-all-done.k_ref.v_ref.q_ref = bf16[16,3,32,512]{3,2,1,0:T(8,128)(2,1)S(1)} async-done(((bf16[16,3,32,512]{3,2,1,0:T(8,128)(2,1)}), bf16[16,3,32,512]{3,2,1,0:T(8,128)(2,1)S(1)}, u32[]{:S(2)}, u32[]{:S(2)}) %all-to-all-start) | async-done | bytes 1572896 | tf_op jit(solution)/shard_map/all_to_all | solution.py:250
  81.5 0.0 copy-done.2
  81.5 1.2 state.1
  82.7 39.0 %all_to_all.20.in_ref = f32[32,24,128]{2,1,0:T(8,128)} all-to-all(f32[32,24,128]{2,1,0:T(8,128)S(1)} %get-tuple-element.8), channel_id=1, replica_groups={{0,16,32,48,64,80,96,112,128,144,160,176,192,208,224,240,256,272,288,30..., dimensions={0} | all-to-all | bytes 786432 | tf_op jit(solution)/shard_map/all_to_all | solution.py:266
  121.8 1.8 scan.1
  123.5 7.3 %all-to-all-start.2 = ((f32[32,16,128]{2,1,0:T(8,128)}), f32[32,16,128]{2,1,0:T(8,128)S(1)}, u32[]{:S(2)}, u32[]{:S(2)}) async-start(f32[32,16,128]{2,1,0:T(8,128)} %scan.1), calls=%async_computation.2 | async-start | bytes 524288 | tf_op jit(solution)/shard_map/all_to_all | solution.py:282
  130.8 0.0 copy-start.1
  130.8 2.9 %near.1.near_ref = f32[4,512,128]{2,1,0:T(8,128)S(1)} custom-call(bf16[16,3,32,512]{3,2,1,0:T(8,128)(2,1)S(1)} %all-to-all-done.k_ref.v_ref.q_ref, bf16[16,3,32,512]{3,2,1,0:T(8,128)(2,1)S(1)} %all-to-all-done.k_ref.v_ref.q_ref, bf16[16,3,32,512]{3,2,1,0:T(8,128)(2,1)S(1)} %all-to-all-done.k_ref.v_ref.q_ref, f32[128,128]{1,0:T(8,128)S(1)} %get-tuple-element.9.rows_ref, ...), custom_call_target="tpu_custom_call" | custom-call | flops 500000000 | bytes 4000000 | tf_op jit(solution)/shard_map/near/pallas_call | solution.py:267
  133.8 12.6 %all-to-all-done.2 = f32[32,16,128]{2,1,0:T(8,128)S(1)} async-done(((f32[32,16,128]{2,1,0:T(8,128)}), f32[32,16,128]{2,1,0:T(8,128)S(1)}, u32[]{:S(2)}, u32[]{:S(2)}) %all-to-all-start.2) | async-done | bytes 262176 | tf_op jit(solution)/shard_map/all_to_all | solution.py:282
  146.4 0.0 copy-done.1
  146.4 2.2 %close.1 = bf16[16,32,512]{2,1,0:T(8,128)(2,1)S(1)} custom-call(s32[2]{0:T(128)S(1)} %pad_add_fusion.place_ref, bf16[16,3,32,512]{3,2,1,0:T(8,128)(2,1)S(1)} %all-to-all-done.k_ref.v_ref.q_ref, f32[4,128,128]{2,1,0:T(8,128)S(1)} %bitcast.4, f32[4,512,128]{2,1,0:T(8,128)S(1)} %near.1.near_ref, f32[128,128]{1,0:T(8,128)S(1)} %get-tuple-element.10.cols_ref, ...), custom_call_target="tpu_custom_call" | custom-call | tf_op jit(solution)/shard_map/close/pallas_call | solution.py:285
  148.6 19.7 %all_to_all.21.in_ref = bf16[16,32,512]{2,1,0:T(8,128)(2,1)} all-to-all(bf16[16,32,512]{2,1,0:T(8,128)(2,1)S(1)} %close.1), channel_id=1, replica_groups={{0,1,2,3,4,5,6,7,8,9,10,11,12,13,14,15},{16,17,18,19,20,21,22,23,24,25,..., dimensions={0} | all-to-all | bytes 1048576 | tf_op jit(solution)/shard_map/all_to_all | solution.py:301
  168.3 17.1 %unpack.1 = bf16[32,8192]{1,0:T(8,128)(2,1)} custom-call(bf16[16,32,512]{2,1,0:T(8,128)(2,1)} %all_to_all.21.in_ref), custom_call_target="tpu_custom_call" | custom-call | tf_op jit(solution)/shard_map/unpack/pallas_call | solution.py:304
Async XLA Ops:
  49.2 10.4 %copy-start = (f32[8,256]{1,0:T(8,128)S(1)}, f32[8,256]{1,0:T(8,128)}, u32[]{:S(2)}) copy-start(f32[8,256]{1,0:T(8,128)} %own_ref.1) | copy-start | bytes 24580
  49.2 32.3 %copy-start.2 = (s32[32]{0:T(128)S(1)}, s32[32]{0:T(128)}, u32[]{:S(2)}) copy-start(s32[32]{0:T(128)} %lengths_ref.1) | copy-start | bytes 388
  49.2 32.3 %all-to-all-start = ((bf16[16,3,32,512]{3,2,1,0:T(8,128)(2,1)}), bf16[16,3,32,512]{3,2,1,0:T(8,128)(2,1)S(1)}, u32[]{:S(2)}, u32[]{:S(2)}) async-start(bf16[16,3,32,512]{3,2,1,0:T(8,128)(2,1)} %pack.1), calls=%async_computation | async-start | bytes 3145728 | tf_op jit(solution)/shard_map/all_to_all | solution.py:250
  59.6 19.4 %collective-permute-start = (f32[8,256]{1,0:T(8,128)S(1)}, f32[8,256]{1,0:T(8,128)S(1)}, u32[]{:S(2)}, u32[]{:S(2)}) collective-permute-start(f32[8,256]{1,0:T(8,128)S(1)} %copy-done), channel_id=1, source_target_pairs={{0,8},{8,0},{16,24},{24,16},{32,40},{40,32},{48,56},{56,48},{64,72... | collective-permute-start | bytes 24584 | tf_op jit(solution)/shard_map/ppermute | solution.py:241
  123.5 22.9 %all-to-all-start.2 = ((f32[32,16,128]{2,1,0:T(8,128)}), f32[32,16,128]{2,1,0:T(8,128)S(1)}, u32[]{:S(2)}, u32[]{:S(2)}) async-start(f32[32,16,128]{2,1,0:T(8,128)} %scan.1), calls=%async_computation.2 | async-start | bytes 524288 | tf_op jit(solution)/shard_map/all_to_all | solution.py:282
  130.8 15.5 %copy-start.1 = (f32[1024]{0:T(1024)S(1)}, f32[1024]{0:T(1024)}, u32[]{:S(2)}) copy-start(f32[1024]{0:T(1024)} %param.11) | copy-start | bytes 12292

commit v2 on v1

--- a/solution.py
+++ b/solution.py
@@ -17,6 +17,7 @@
 SEG = CH * NC
 GROUP = 16
 ROWS = 16
+PIECE = ROWS + 1
 VMEM_LIMIT = 48 * 1024 * 1024
 
 
@@ -36,37 +37,15 @@
     return jnp.dot(a, b, preferred_element_type=F32)
 
 
-def pack_kernel(q_ref, k_ref, v_ref, out_ref, sems):
-    copies = []
-    for place in range(GROUP):
-        column = (2 * (place % 8) + place // 8) * NH * DH
-        for which, ref in enumerate((q_ref, k_ref, v_ref)):
-            copies.append(
-                pltpu.make_async_copy(
-                    ref.at[:, pl.ds(column, NH * DH)],
-                    out_ref.at[place, which],
-                    sems.at[place, which],
-                )
-            )
-    for copy in copies:
-        copy.start()
-    for copy in copies:
-        copy.wait()
-
-
-def unpack_kernel(in_ref, out_ref, sems):
-    copies = []
-    for place in range(GROUP):
-        column = (2 * (place % 8) + place // 8) * NH * DH
-        copies.append(
-            pltpu.make_async_copy(
-                in_ref.at[place], out_ref.at[:, pl.ds(column, NH * DH)], sems.at[place]
-            )
-        )
-    for copy in copies:
-        copy.start()
-    for copy in copies:
-        copy.wait()
+def pack_kernel(q_ref, k_ref, v_ref, out_ref):
+    for which, ref in enumerate((q_ref, k_ref, v_ref)):
+        for part in range(4):
+            out_ref[part % 2, part // 2, which] = ref[:, part * NH * DH : (part + 1) * NH * DH]
+
+
+def unpack_kernel(in_ref, out_ref):
+    for part in range(4):
+        out_ref[:, part * NH * DH : (part + 1) * NH * DH] = in_ref[part % 2, part // 2]
 
 
 def pick_heads(tile, half):
@@ -142,10 +121,13 @@
         weighted = key_part.T.astype(F32) * weight
         both = dot(jnp.concatenate(split2(weighted), axis=0), value_part)
         state = both[:DH] + both[DH:]
-        factor = jnp.broadcast_to(before[NC][head : head + 1], (8, DH))
         for piece in range(DH // ROWS):
-            send_ref[head * (DH // ROWS) + piece, :ROWS] = state[piece * ROWS : (piece + 1) * ROWS]
-            send_ref[head * (DH // ROWS) + piece, ROWS:] = factor
+            place = head * (DH // ROWS) + piece
+            for row in range(ROWS):
+                send_ref[place, :, row * DH : (row + 1) * DH] = state[
+                    piece * ROWS + row : piece * ROWS + row + 1
+                ]
+            send_ref[place, :, ROWS * DH :] = before[NC][head : head + 1]
 
 
 def near_kernel(q_ref, k_ref, v_ref, rows_ref, cols_ref, near_ref):
@@ -184,11 +166,11 @@
 
 
 def scan_kernel(in_ref, out_ref):
-    state = jnp.zeros((ROWS, DH), F32)
-    for segment in range(in_ref.shape[0]):
+    state = jnp.zeros((1, ROWS * DH), F32)
+    for segment in range(out_ref.shape[0]):
         out_ref[segment] = state
-        factor = in_ref[segment, ROWS : ROWS + 1]
-        state = state * factor + in_ref[segment, :ROWS]
+        factor = jnp.concatenate([in_ref[segment, :, ROWS * DH :]] * ROWS, axis=1)
+        state = state * factor + in_ref[segment, :, : ROWS * DH]
 
 
 def close_kernel(place_ref, q_ref, state_ref, near_ref, cols_ref, gain_ref, out_ref):
@@ -209,9 +191,7 @@
             out_ref[4 * c : 4 * c + 4, :, at] = normed.astype(BF16).reshape(4, CH // 4, DH)
 
 
-VMEM = pl.BlockSpec(memory_space=pltpu.VMEM)
 SMEM = pl.BlockSpec(memory_space=pltpu.SMEM)
-ANY = pl.BlockSpec(memory_space=pl.ANY)
 PARAMS = pltpu.CompilerParams(vmem_limit_bytes=VMEM_LIMIT)
 
 
@@ -241,25 +221,26 @@
     other_decay = lax.ppermute(log_decay, "seq", [(s, s ^ 1) for s in range(seq_size)])
     sent = pl.pallas_call(
         pack_kernel,
-        out_shape=shaped((GROUP, 3, tokens, NH * DH), BF16),
-        in_specs=[ANY] * 3,
-        out_specs=ANY,
-        scratch_shapes=[pltpu.SemaphoreType.DMA((GROUP, 3))],
+        out_shape=shaped((2, 8, 3, tokens, NH * DH), BF16),
+        grid=(4,),
+        in_specs=[pl.BlockSpec((tokens, 4 * NH * DH), lambda i: (0, i))] * 3,
+        out_specs=pl.BlockSpec((2, 2, 3, tokens, NH * DH), lambda i: (0, i, 0, 0, 0)),
+        compiler_params=PARAMS,
         name="pack",
-    )(queries, keys, values)
+    )(queries, keys, values).reshape(GROUP, 3, tokens, NH * DH)
     parts = lax.all_to_all(
         sent, ("seq", "head"), 0, 0, axis_index_groups=token_groups, tiled=True
     )
     own, rows, cols = pl.pallas_call(
         state_kernel,
         out_shape=(
-            shaped((pieces, ROWS + 8, DH)),
+            shaped((pieces, 1, PIECE * DH)),
             shaped((128, CH)),
             shaped((CH, 128)),
         ),
         grid=(1,),
         in_specs=[SMEM, SMEM, whole(8, SEG // PAIR), whole(8, SEG // PAIR), part_spec(1), part_spec(2)],
-        out_specs=(whole(pieces, ROWS + 8, DH), whole(128, CH), whole(CH, 128)),
+        out_specs=(whole(pieces, 1, PIECE * DH), whole(128, CH), whole(CH, 128)),
         compiler_params=PARAMS,
         name="state",
     )(place, doc_lengths, log_decay, other_decay, parts, parts)
@@ -276,7 +257,7 @@
     )(parts, parts, parts, rows, cols)
     prefixes = pl.pallas_call(
         scan_kernel,
-        out_shape=shaped((segments, ROWS, DH)),
+        out_shape=shaped((segments, 1, ROWS * DH)),
         name="scan",
     )(gathered)
     incoming = lax.all_to_all(
@@ -304,11 +285,12 @@
     return pl.pallas_call(
         unpack_kernel,
         out_shape=shaped((tokens, GROUP * NH * DH), BF16),
-        in_specs=[ANY],
-        out_specs=ANY,
-        scratch_shapes=[pltpu.SemaphoreType.DMA((GROUP,))],
+        grid=(4,),
+        in_specs=[pl.BlockSpec((2, 2, tokens, NH * DH), lambda i: (0, i, 0, 0))],
+        out_specs=pl.BlockSpec((tokens, 4 * NH * DH), lambda i: (0, i)),
+        compiler_params=PARAMS,
         name="unpack",
-    )(returned)
+    )(returned.reshape(2, 8, tokens, NH * DH))
 
 
 def solution(mesh):

time: 186 us -> 124 us (0.67)
  Pallas kernels: 74.4 us -> 11.5 us
  local copies, waits for them, and re-layouts: 0.02 us -> 3.14 us
  blocking collectives: 58.8 us -> 55.7 us
    pallas_call x3, Pallas kernels: 52.2 us -> 4.98 us  [the longest x1 1.9 us: local(): pl.pallas_call(scan_kernel, out_shape=shaped((segments, 1, ROWS * DH)), n...]
    pallas_call x1, Pallas kernels: 17.1 us -> 1.42 us  [local(): pl.pallas_call(unpack_kernel, out_shape=shaped((tokens, GROUP * NH * DH),...]
    all_to_all x1, blocking collectives: 39 us -> 33.9 us  [local(): lax.all_to_all(own, 'seq', 0, 0, axis_index_groups=scan_groups, tiled=True)]
    unnamed x6 -> x12, local copies, waits for them, and re-layouts: 0.02 us -> 3.14 us
    all_to_all x1, blocking collectives: 19.7 us -> 21.8 us  [local(): lax.all_to_all(normed, ('seq', 'head'), 0, 0, axis_index_groups=token_gro...]
where the time goes in v2:
time: 124 us; the launch traced here: 123 us
  blocking collectives  55.7 us (45%)
  waiting for transfers between devices  31.6 us (25%)
  starting transfers between devices  21.1 us (17%)
  Pallas kernels  11.5 us (9%)
  local copies, waits for them, and re-layouts  3.14 us (3%)
    all_to_all x1, blocking collectives, local(): lax.all_to_all(own, 'seq', 0, 0, axis_index_groups=scan_groups, tiled=True)  33.9 us
    all_to_all x1, blocking collectives, local(): lax.all_to_all(normed, ('seq', 'head'), 0, 0, axis_index_groups=token_gro...  21.8 us
    ppermute x1, waiting for transfers between devices, local(): lax.ppermute(log_decay, 'seq', [(s, s ^ 1) for s in range(seq_size)])  16 us
    all_to_all x1, waiting for transfers between devices, local(): lax.all_to_all(prefixes, 'seq', 0, 0, axis_index_groups=scan_groups, tile...  13.1 us
    all_to_all x1, starting transfers between devices, local(): lax.all_to_all(sent, ('seq', 'head'), 0, 0, axis_index_groups=token_group...  10.5 us
    all_to_all x1, starting transfers between devices, local(): lax.all_to_all(prefixes, 'seq', 0, 0, axis_index_groups=scan_groups, tile...  7.23 us
    ppermute x1, starting transfers between devices, local(): lax.ppermute(log_decay, 'seq', [(s, s ^ 1) for s in range(seq_size)])  3.34 us
    unnamed x12, local copies, waits for them, and re-layouts  3.14 us
  transfers between devices with their start and end apart: 3, of which 3 were waited for; matrix products, arithmetic and copies ran while one was open for 0% of the time, Pallas kernels for 2%

profile of v2, /device:TPU:1, one launch (start us, length us, event | category | flops | bytes accessed | tf_op | source)
XLA Modules:
  0.0 123.2 jit_solution(7648093516745902213)
XLA Ops:
  0.0 0.0 copy-start
  0.0 1.0 copy-done
  1.0 0.0 copy-start.1
  1.0 1.0 copy-done.1
  2.1 0.0 copy-start.2
  2.1 1.0 copy-done.2
  3.1 1.8 %pack.1 = bf16[2,8,3,32,512]{4,3,2,1,0:T(8,128)(2,1)} custom-call(bf16[32,8192]{1,0:T(8,128)(2,1)S(1)} %copy-done, bf16[32,8192]{1,0:T(8,128)(2,1)S(1)} %copy-done.1, bf16[32,8192]{1,0:T(8,128)(2,1)S(1)} %copy-done.2), custom_call_target="tpu_custom_call" | custom-call | tf_op jit(solution)/shard_map/pack/pallas_call | solution.py:222
  4.9 0.0 copy-start.3
  4.9 0.0 copy-start.5
  4.9 10.5 %all-to-all-start = ((bf16[16,3,32,512]{3,2,1,0:T(8,128)(2,1)}), bf16[16,3,32,512]{3,2,1,0:T(8,128)(2,1)S(1)}, u32[]{:S(2)}, u32[]{:S(2)}) async-start(bf16[16,3,32,512]{3,2,1,0:T(8,128)(2,1)} %bitcast.2), calls=%async_computation | async-start | bytes 3145728 | tf_op jit(solution)/shard_map/all_to_all | solution.py:231
  15.5 0.0 copy-done.3
  15.5 3.3 %collective-permute-start = (f32[8,256]{1,0:T(8,128)S(1)}, f32[8,256]{1,0:T(8,128)S(1)}, u32[]{:S(2)}, u32[]{:S(2)}) collective-permute-start(f32[8,256]{1,0:T(8,128)S(1)} %copy-done.3), channel_id=1, source_target_pairs={{0,8},{8,0},{16,24},{24,16},{32,40},{40,32},{48,56},{56,48},{64,72... | collective-permute-start | bytes 24584 | tf_op jit(solution)/shard_map/ppermute | solution.py:221
  18.8 0.1 pad_add_fusion.place_ref
  18.9 16.0 %collective-permute-done.other_ref = f32[8,256]{1,0:T(8,128)S(1)} collective-permute-done((f32[8,256]{1,0:T(8,128)S(1)}, f32[8,256]{1,0:T(8,128)S(1)}, u32[]{:S(2)}, u32[]{:S(2)}) %collective-permute-start) | collective-permute-done | bytes 8224 | tf_op jit(solution)/shard_map/ppermute | solution.py:221
  34.9 2.5 %all-to-all-done.k_ref.v_ref.q_ref = bf16[16,3,32,512]{3,2,1,0:T(8,128)(2,1)S(1)} async-done(((bf16[16,3,32,512]{3,2,1,0:T(8,128)(2,1)}), bf16[16,3,32,512]{3,2,1,0:T(8,128)(2,1)S(1)}, u32[]{:S(2)}, u32[]{:S(2)}) %all-to-all-start) | async-done | bytes 1572896 | tf_op jit(solution)/shard_map/all_to_all | solution.py:231
  37.3 0.0 copy-done.5
  37.3 1.3 %state.1 = (f32[32,1,2176]{2,1,0:T(1,128)S(1)}, f32[128,128]{1,0:T(8,128)S(1)}, f32[128,128]{1,0:T(8,128)S(1)}) custom-call(s32[2]{0:T(128)S(1)} %pad_add_fusion.place_ref, s32[32]{0:T(128)S(1)} %copy-done.5, f32[8,256]{1,0:T(8,128)S(1)} %copy-done.3, f32[8,256]{1,0:T(8,128)S(1)} %collective-permute-done.other_ref, ...), custom_call_target="tpu_custom_call" | custom-call | tf_op jit(solution)/shard_map/state/pallas_call | solution.py:234
  38.6 33.9 %all_to_all.20.in_ref = f32[32,1,2176]{2,1,0:T(1,128)} all-to-all(f32[32,1,2176]{2,1,0:T(1,128)S(1)} %get-tuple-element.8), channel_id=1, replica_groups={{0,16,32,48,64,80,96,112,128,144,160,176,192,208,224,240,256,272,288,30..., dimensions={0} | all-to-all | bytes 557056 | tf_op jit(solution)/shard_map/all_to_all | solution.py:247
  72.5 1.9 %scan.1 = f32[32,1,2048]{2,1,0:T(1,128)} custom-call(f32[32,1,2176]{2,1,0:T(1,128)} %all_to_all.20.in_ref), custom_call_target="tpu_custom_call" | custom-call | tf_op jit(solution)/shard_map/scan/pallas_call | solution.py:258
  74.4 7.2 %all-to-all-start.2 = ((f32[32,1,2048]{2,1,0:T(1,128)}), f32[32,1,2048]{2,1,0:T(1,128)S(1)}, u32[]{:S(2)}, u32[]{:S(2)}) async-start(f32[32,1,2048]{2,1,0:T(1,128)} %scan.1), calls=%async_computation.2 | async-start | bytes 524288 | tf_op jit(solution)/shard_map/all_to_all | solution.py:263
  81.7 0.0 copy-start.4
  81.7 2.9 %near.1.near_ref = f32[4,512,128]{2,1,0:T(8,128)S(1)} custom-call(bf16[16,3,32,512]{3,2,1,0:T(8,128)(2,1)S(1)} %all-to-all-done.k_ref.v_ref.q_ref, bf16[16,3,32,512]{3,2,1,0:T(8,128)(2,1)S(1)} %all-to-all-done.k_ref.v_ref.q_ref, bf16[16,3,32,512]{3,2,1,0:T(8,128)(2,1)S(1)} %all-to-all-done.k_ref.v_ref.q_ref, f32[128,128]{1,0:T(8,128)S(1)} %get-tuple-element.9.rows_ref, ...), custom_call_target="tpu_custom_call" | custom-call | flops 500000000 | bytes 4000000 | tf_op jit(solution)/shard_map/near/pallas_call | solution.py:248
  84.6 13.1 %all-to-all-done.2 = f32[32,1,2048]{2,1,0:T(1,128)S(1)} async-done(((f32[32,1,2048]{2,1,0:T(1,128)}), f32[32,1,2048]{2,1,0:T(1,128)S(1)}, u32[]{:S(2)}, u32[]{:S(2)}) %all-to-all-start.2) | async-done | bytes 262176 | tf_op jit(solution)/shard_map/all_to_all | solution.py:263
  97.8 0.0 copy-done.4
  97.8 2.2 %close.1 = bf16[16,32,512]{2,1,0:T(8,128)(2,1)S(1)} custom-call(s32[2]{0:T(128)S(1)} %pad_add_fusion.place_ref, bf16[16,3,32,512]{3,2,1,0:T(8,128)(2,1)S(1)} %all-to-all-done.k_ref.v_ref.q_ref, f32[4,128,128]{2,1,0:T(8,128)S(1)} %bitcast.7, f32[4,512,128]{2,1,0:T(8,128)S(1)} %near.1.near_ref, f32[128,128]{1,0:T(8,128)S(1)} %get-tuple-element.10.cols_ref, ...), custom_call_target="tpu_custom_call" | custom-call | tf_op jit(solution)/shard_map/close/pallas_call | solution.py:266
  99.9 21.8 %all_to_all.21 = bf16[16,32,512]{2,1,0:T(8,128)(2,1)S(1)} all-to-all(bf16[16,32,512]{2,1,0:T(8,128)(2,1)S(1)} %close.1), channel_id=1, replica_groups={{0,1,2,3,4,5,6,7,8,9,10,11,12,13,14,15},{16,17,18,19,20,21,22,23,24,25,..., dimensions={0} | all-to-all | bytes 1048576 | tf_op jit(solution)/shard_map/all_to_all | solution.py:282
  121.8 1.4 %unpack.1 = bf16[32,8192]{1,0:T(8,128)(2,1)} custom-call(bf16[2,8,32,512]{3,2,1,0:T(8,128)(2,1)S(1)} %bitcast.6), custom_call_target="tpu_custom_call" | custom-call | tf_op jit(solution)/shard_map/unpack/pallas_call | solution.py:285
Async XLA Ops:
  0.0 1.0 copy-start
  1.0 1.0 copy-start.1
  2.1 1.0 copy-start.2
  4.9 10.5 %copy-start.3 = (f32[8,256]{1,0:T(8,128)S(1)}, f32[8,256]{1,0:T(8,128)}, u32[]{:S(2)}) copy-start(f32[8,256]{1,0:T(8,128)} %own_ref.1) | copy-start | bytes 24580
  4.9 32.4 %copy-start.5 = (s32[32]{0:T(128)S(1)}, s32[32]{0:T(128)}, u32[]{:S(2)}) copy-start(s32[32]{0:T(128)} %lengths_ref.1) | copy-start | bytes 388
  4.9 32.4 %all-to-all-start = ((bf16[16,3,32,512]{3,2,1,0:T(8,128)(2,1)}), bf16[16,3,32,512]{3,2,1,0:T(8,128)(2,1)S(1)}, u32[]{:S(2)}, u32[]{:S(2)}) async-start(bf16[16,3,32,512]{3,2,1,0:T(8,128)(2,1)} %bitcast.2), calls=%async_computation | async-start | bytes 3145728 | tf_op jit(solution)/shard_map/all_to_all | solution.py:231
  15.5 19.4 %collective-permute-start = (f32[8,256]{1,0:T(8,128)S(1)}, f32[8,256]{1,0:T(8,128)S(1)}, u32[]{:S(2)}, u32[]{:S(2)}) collective-permute-start(f32[8,256]{1,0:T(8,128)S(1)} %copy-done.3), channel_id=1, source_target_pairs={{0,8},{8,0},{16,24},{24,16},{32,40},{40,32},{48,56},{56,48},{64,72... | collective-permute-start | bytes 24584 | tf_op jit(solution)/shard_map/ppermute | solution.py:221
  74.4 23.3 %all-to-all-start.2 = ((f32[32,1,2048]{2,1,0:T(1,128)}), f32[32,1,2048]{2,1,0:T(1,128)S(1)}, u32[]{:S(2)}, u32[]{:S(2)}) async-start(f32[32,1,2048]{2,1,0:T(1,128)} %scan.1), calls=%async_computation.2 | async-start | bytes 524288 | tf_op jit(solution)/shard_map/all_to_all | solution.py:263
  81.7 16.1 %copy-start.4 = (f32[1024]{0:T(1024)S(1)}, f32[1024]{0:T(1024)}, u32[]{:S(2)}) copy-start(f32[1024]{0:T(1024)} %param.11) | copy-start | bytes 12292

commit v3 on v1

v3 whole, which is shorter than its diff:
```python
import functools

import jax
import jax.numpy as jnp
from jax import lax
from jax.experimental import pallas as pl
from jax.experimental.pallas import tpu as pltpu
from jax.sharding import PartitionSpec as P

F32 = jnp.float32
BF16 = jnp.bfloat16
DH = 128
CH = 128
NC = 4
PAIR = 2
NH = 4
SEG = CH * NC
GROUP = 16
XS = 4
ROWS = 16
PIECE = ROWS + 1
VMEM_LIMIT = 16 * 1024 * 1024


def split2(x):
    high = x.astype(BF16)
    return high, (x - high.astype(F32)).astype(BF16)


def split3(x):
    high = x.astype(BF16)
    rest = x - high.astype(F32)
    mid = rest.astype(BF16)
    return high, mid, (rest - mid.astype(F32)).astype(BF16)


def dot(a, b):
    return jnp.dot(a, b, preferred_element_type=F32)


def pack_kernel(k_ref, v_ref, out_ref, taken, ready, in_sems, out_sems):
    span = NH * DH
    refs = (k_ref, v_ref)
    loads, stores = [], []
    for part in range(4):
        columns = pl.ds(4 * part * span, 4 * span)
        loads.append(
            [
                pltpu.make_async_copy(
                    ref.at[:, columns], taken.at[which, :, columns], in_sems.at[part, which]
                )
                for which, ref in enumerate(refs)
            ]
        )
        stores.append(
            [
                pltpu.make_async_copy(
                    ready.at[pl.ds(8 * half + 2 * part, 2)],
                    out_ref.at[pl.ds(8 * half + 2 * part, 2)],
                    out_sems.at[part, half],
                )
                for half in range(2)
            ]
        )
    for group in loads:
        for copy in group:
            copy.start()
    for part in range(4):
        for which in range(2):
            loads[part][which].wait()
            for block in range(4):
                column = (4 * part + block) * span
                place = 8 * (block % 2) + 2 * part + block // 2
                ready[place, which] = taken[which, :, column : column + span]
        for copy in stores[part]:
            copy.start()
    for group in stores:
        for copy in group:
            copy.wait()


def fold_kernel(place_ref, q_ref, keep_ref, send_ref, sems):
    across, core = place_ref[2], place_ref[3]
    width = 2 * NH * DH
    copies = []
    for turn in range(XS):
        base = 2 * lax.rem(across + turn, XS)
        for which, ref in enumerate((keep_ref, send_ref)):
            goal = base + (core if which == 0 else 1 - core)
            columns = pl.ds(pl.multiple_of(goal * width, width), width)
            copies.append(
                pltpu.make_async_copy(q_ref.at[:, columns], ref.at[turn], sems.at[turn, which])
            )
    for copy in copies:
        copy.start()
    for copy in copies:
        copy.wait()


def weave_kernel(place_ref, keep_ref, other_ref, *slab_refs):
    core = place_ref[3]
    for turn, slab_ref in enumerate(slab_refs):
        slab_ref[core] = keep_ref[turn]
        slab_ref[1 - core] = other_ref[turn]


def regroup_kernel(place_ref, *refs):
    half, across = place_ref[1], place_ref[2]
    slab_refs, (keep_ref, send_ref) = refs[:XS], refs[XS:]
    span = NH * DH
    mine = pl.ds(pl.multiple_of(half * span, span), span)
    theirs = pl.ds(pl.multiple_of((1 - half) * span, span), span)
    for turn, slab_ref in enumerate(slab_refs):
        origin = lax.rem(across + XS - turn, XS)
        for core in range(2):
            keep_ref[2 * origin + core] = slab_ref[core, :, mine]
            send_ref[2 * origin + core] = slab_ref[core, :, theirs]


def unpack_kernel(in_ref, out_ref, ready, sems):
    tokens = in_ref.shape[1]
    span = NH * DH
    copies = []
    for row in range(tokens // 8):
        for place in range(GROUP):
            column = (2 * (place % 8) + place // 8) * span
            ready[8 * row : 8 * row + 8, column : column + span] = in_ref[
                place, 8 * row : 8 * row + 8, :
            ]
        rows = pl.ds(8 * row, 8)
        copies.append(pltpu.make_async_copy(ready.at[rows, :], out_ref.at[rows, :], sems.at[row]))
        copies[-1].start()
    for copy in copies:
        copy.wait()


def pick_heads(tile, half):
    return jnp.where(half == 0, tile, pltpu.roll(tile, 4, axis=0))


def state_kernel(place_ref, lengths_ref, own_ref, other_ref, part_ref, out_ref, rows_ref, cols_ref, send_ref, sems):
    segment, half = place_ref[0], place_ref[1]
    own, other = own_ref[...], other_ref[...]
    first = jnp.where(half == 0, own, other)
    second = jnp.where(half == 0, other, own)
    decay = jnp.concatenate(
        [
            pick_heads(part[:, i * CH : (i + 1) * CH], half)
            for part in (first, second)
            for i in range(2)
        ],
        axis=0,
    )
    upper = (
        lax.broadcasted_iota(jnp.int32, (CH, CH), 0) <= lax.broadcasted_iota(jnp.int32, (CH, CH), 1)
    ).astype(BF16)
    high, mid, low = split3(decay)
    sums = dot(high, upper) + (dot(mid, upper) + dot(low, upper))

    lane = lax.broadcasted_iota(jnp.int32, (8, CH), 1)
    start = segment * SEG
    spots = [jnp.full((8, CH), start - 1, jnp.int32)] + [start + c * CH + lane for c in range(NC)]
    ids = [jnp.zeros((8, CH), jnp.int32) for _ in spots]
    end = jnp.int32(0)
    for d in range(lengths_ref.shape[0]):
        end = end + lengths_ref[d]
        ids = [i + (end <= s).astype(jnp.int32) for i, s in zip(ids, spots)]

    def last(tile):
        return jnp.broadcast_to(tile[:, CH - 1 : CH], (8, CH))

    prior = ids[0]
    tails, leads, carries = [], [], []
    for c in range(NC):
        local, here = sums[8 * c : 8 * c + 8], ids[c + 1]
        total, closing = last(local), last(here)
        tails.append(jnp.where(here == closing, jnp.exp(total - local), 0.0))
        leads.append(jnp.where(here == prior, jnp.exp(local), 0.0))
        carries.append(jnp.where(closing == prior, jnp.exp(total), 0.0))
        prior = closing
    before = [jnp.ones((8, CH), F32)]
    for c in range(NC):
        before.append(before[-1] * carries[c])
    after = [jnp.ones((8, CH), F32)]
    for c in range(NC - 1, 0, -1):
        after.append(after[-1] * carries[c])
    after = after[::-1]
    rows_ref[0:32] = sums
    rows_ref[32:64] = jnp.concatenate(tails, axis=0)
    rows_ref[64:96] = jnp.concatenate(carries, axis=0)
    rows_ref[96:128] = jnp.concatenate([i.astype(F32) for i in ids[1:]], axis=0)
    table = jnp.concatenate(
        [sums]
        + leads
        + [lead * b for lead, b in zip(leads, before)]
        + [i.astype(F32) for i in ids[1:]],
        axis=0,
    )
    cols_ref[...] = table.T

    full_tails = [t * a for t, a in zip(tails, after)]
    copies = []
    for head in range(NH):
        at = slice(head * DH, (head + 1) * DH)
        key_part = part_ref[:, 0, :, at].reshape(SEG, DH)
        value_part = part_ref[:, 1, :, at].reshape(SEG, DH)
        weight = jnp.concatenate([t[head : head + 1] for t in full_tails], axis=1)
        weighted = key_part.T.astype(F32) * weight
        both = dot(jnp.concatenate(split2(weighted), axis=0), value_part)
        state = both[:DH] + both[DH:]
        for piece in range(DH // ROWS):
            top = (head * (DH // ROWS) + piece) * PIECE
            send_ref[top : top + ROWS] = state[piece * ROWS : (piece + 1) * ROWS]
            send_ref[top + ROWS : top + PIECE] = before[NC][head : head + 1]
        done = pl.ds(head * (DH // ROWS) * PIECE, (DH // ROWS) * PIECE)
        copies.append(pltpu.make_async_copy(send_ref.at[done], out_ref.at[done], sems.at[head]))
        copies[-1].start()
    for copy in copies:
        copy.wait()


def near_kernel(
    place_ref, own_ref, other_ref, part_ref, rows_ref, cols_ref, gain_in_ref, near_ref, scaled_ref, gain_ref
):
    half = place_ref[1]
    gain_ref[...] = pick_heads(gain_in_ref[...], half)
    order = lax.broadcasted_iota(jnp.int32, (CH, CH), 0) >= lax.broadcasted_iota(
        jnp.int32, (CH, CH), 1
    )
    cols = cols_ref[...]
    masks = []
    for c in range(NC):
        ids_row = rows_ref[96 + 8 * c : 97 + 8 * c]
        ids_col = cols[:, 96 + 8 * c : 97 + 8 * c]
        masks.append(order & (ids_col == ids_row))
    for head in range(NH):
        at = slice(head * DH, (head + 1) * DH)
        state = None
        for c in range(NC):
            part = slice(4 * c, 4 * c + 4)
            row = 8 * c + head
            blocks = slice(4 * (c % 2), 4 * (c % 2) + 4)
            query = jnp.where(
                half == c // 2, own_ref[blocks, :, at], other_ref[blocks, :, at]
            ).reshape(CH, DH)
            key_part = part_ref[part, 0, :, at].reshape(CH, DH)
            value_part = part_ref[part, 1, :, at].reshape(CH, DH)
            keys_across = key_part.T
            gaps = cols[:, row : row + 1] - rows_ref[row : row + 1]
            weights = jnp.where(masks[c], jnp.exp(jnp.where(masks[c], gaps, 0.0)), 0.0)
            high, low = split2(dot(query, keys_across) * weights)
            mixed = dot(high, value_part) + dot(low, value_part)
            if c:
                both = dot(query, jnp.concatenate(split2(state), axis=1))
                mixed = mixed + (both[:, :DH] + both[:, DH:]) * cols[:, 32 + row : 33 + row]
            near_ref[head, c * CH : (c + 1) * CH] = mixed
            high, low = split2(query.astype(F32) * cols[:, 64 + row : 65 + row])
            scaled_ref[head, c * CH : (c + 1) * CH, :DH] = high
            scaled_ref[head, c * CH : (c + 1) * CH, DH:] = low
            if c < NC - 1:
                weighted = keys_across.astype(F32) * rows_ref[32 + row : 33 + row]
                both = dot(jnp.concatenate(split2(weighted), axis=0), value_part)
                own = both[:DH] + both[DH:]
                state = own if c == 0 else own + state * rows_ref[64 + row : 65 + row]


def scan_kernel(in_ref, out_ref, ready, sems):
    segments = out_ref.shape[0]
    run = segments // 4
    state = jnp.zeros((ROWS, DH), F32)
    copies = []
    for segment in range(segments):
        ready[segment] = state
        top = segment * PIECE
        state = state * in_ref[top + ROWS : top + PIECE] + in_ref[top : top + ROWS]
        if segment % run == run - 1:
            done = pl.ds(segment + 1 - run, run)
            copies.append(
                pltpu.make_async_copy(ready.at[done], out_ref.at[done], sems.at[segment // run])
            )
            copies[-1].start()
    for copy in copies:
        copy.wait()


def close_kernel(scaled_ref, state_ref, near_ref, gain_ref, out_ref):
    averaging = jnp.full((2 * DH, DH), 1.0 / DH, BF16)
    for head in range(NH):
        high, low = split2(state_ref[head])
        right = jnp.concatenate(
            [
                jnp.concatenate([high, low], axis=1),
                jnp.concatenate([high, jnp.zeros_like(low)], axis=1),
            ],
            axis=0,
        )
        both = dot(scaled_ref[head], right)
        mixed = near_ref[head] + (both[:, :DH] + both[:, DH:])
        square = dot(jnp.concatenate(split2(mixed * mixed), axis=1), averaging)
        normed = mixed * lax.rsqrt(square + 1e-06) * gain_ref[head : head + 1]
        out_ref[:, :, head * DH : (head + 1) * DH] = normed.astype(BF16).reshape(
            GROUP, SEG // GROUP, DH
        )


SMEM = pl.BlockSpec(memory_space=pltpu.SMEM)
VMEM = pl.BlockSpec(memory_space=pltpu.VMEM)
ANY = pl.BlockSpec(memory_space=pl.ANY)
PARAMS = pltpu.CompilerParams(vmem_limit_bytes=VMEM_LIMIT)
WIDE = pltpu.CompilerParams(vmem_limit_bytes=60 * 1024 * 1024)


def shaped(shape, kind=F32):
    return jax.ShapeDtypeStruct(shape, kind)


def local(seq_size, head_size, queries, keys, values, log_decay, doc_lengths, gain):
    tokens = queries.shape[0]
    span = NH * DH
    segments = seq_size // PAIR
    pieces = NH * DH // ROWS
    seq, head = lax.axis_index("seq"), lax.axis_index("head")
    place = jnp.stack([seq // PAIR, seq % PAIR, head // 2, head % 2]).astype(jnp.int32)
    token_groups = [
        [g * GROUP + i for i in range(GROUP)] for g in range(seq_size * head_size // GROUP)
    ]
    scan_groups = [[g * PAIR + i for g in range(segments)] for i in range(PAIR)]
    pairs = [(s, s ^ 1) for s in range(seq_size)]

    other_decay = lax.ppermute(log_decay, "seq", pairs)
    sent = pl.pallas_call(
        pack_kernel,
        out_shape=shaped((GROUP, 2, tokens, span), BF16),
        in_specs=[ANY] * 2,
        out_specs=ANY,
        scratch_shapes=[
            pltpu.VMEM((2, tokens, GROUP * span), BF16),
            pltpu.VMEM((GROUP, 2, tokens, span), BF16),
            pltpu.SemaphoreType.DMA((4, 2)),
            pltpu.SemaphoreType.DMA((4, 2)),
        ],
        compiler_params=WIDE,
        name="pack",
    )(keys, values)
    parts = lax.all_to_all(
        sent, ("seq", "head"), 0, 0, axis_index_groups=token_groups, tiled=True
    )

    kept, folded = pl.pallas_call(
        fold_kernel,
        out_shape=[shaped((XS, tokens, 2 * span), BF16)] * 2,
        in_specs=[SMEM, ANY],
        out_specs=[VMEM] * 2,
        scratch_shapes=[pltpu.SemaphoreType.DMA((XS, 2))],
        compiler_params=PARAMS,
        name="fold",
    )(place, queries)
    unfolded = lax.ppermute(folded, "head", [(h, h ^ 1) for h in range(head_size)])
    slabs = pl.pallas_call(
        weave_kernel,
        out_shape=[shaped((2, tokens, 2 * span), BF16)] * XS,
        in_specs=[SMEM, VMEM, VMEM],
        out_specs=[VMEM] * XS,
        compiler_params=PARAMS,
        name="weave",
    )(place, kept, unfolded)

    own, rows, cols = pl.pallas_call(
        state_kernel,
        out_shape=(
            shaped((pieces * PIECE, DH)),
            shaped((128, CH)),
            shaped((CH, 128)),
        ),
        in_specs=[SMEM, SMEM, VMEM, VMEM, VMEM],
        out_specs=(ANY, VMEM, VMEM),
        scratch_shapes=[
            pltpu.VMEM((pieces * PIECE, DH), F32),
            pltpu.SemaphoreType.DMA((NH,)),
        ],
        compiler_params=PARAMS,
        name="state",
    )(place, doc_lengths, log_decay, other_decay, parts)
    slabs, own = lax.optimization_barrier((slabs, own))
    gathered = lax.all_to_all(
        own.reshape(pieces, 1, PIECE * DH), "seq", 0, 0, axis_index_groups=scan_groups, tiled=True
    ).reshape(pieces * PIECE, DH)
    turned = [slabs[0]] + [
        lax.ppermute(
            slabs[turn],
            "head",
            [(h, (h // 2 + turn) % XS * 2 + h % 2) for h in range(head_size)],
        )
        for turn in range(1, XS)
    ]
    kept_queries, leaving = pl.pallas_call(
        regroup_kernel,
        out_shape=[shaped((2 * XS, tokens, span), BF16)] * 2,
        in_specs=[SMEM] + [VMEM] * XS,
        out_specs=[VMEM] * 2,
        compiler_params=PARAMS,
        name="regroup",
    )(place, *turned)
    gathered, kept_queries, leaving = lax.optimization_barrier((gathered, kept_queries, leaving))
    prefixes = pl.pallas_call(
        scan_kernel,
        out_shape=shaped((segments, ROWS, DH)),
        in_specs=[VMEM],
        out_specs=ANY,
        scratch_shapes=[
            pltpu.VMEM((segments, ROWS, DH), F32),
            pltpu.SemaphoreType.DMA((4,)),
        ],
        compiler_params=PARAMS,
        name="scan",
    )(gathered)
    incoming = lax.all_to_all(
        prefixes, "seq", 0, 0, axis_index_groups=scan_groups, tiled=True
    ).reshape(NH, DH, DH)
    arriving = lax.ppermute(leaving, "seq", pairs)
    near, scaled, gains = pl.pallas_call(
        near_kernel,
        out_shape=(
            shaped((NH, SEG, DH)),
            shaped((NH, SEG, 2 * DH), BF16),
            shaped((8, DH)),
        ),
        in_specs=[SMEM] + [VMEM] * 6,
        out_specs=(VMEM, VMEM, VMEM),
        compiler_params=PARAMS,
        cost_estimate=pl.CostEstimate(flops=500000000, transcendentals=300000, bytes_accessed=4000000),
        name="near",
    )(place, kept_queries, arriving, parts, rows, cols, gain.reshape(8, DH))
    normed = pl.pallas_call(
        close_kernel,
        out_shape=shaped((GROUP, tokens, span), BF16),
        in_specs=[VMEM] * 4,
        out_specs=VMEM,
        compiler_params=PARAMS,
        name="close",
    )(scaled, incoming, near, gains)
    returned = lax.all_to_all(
        normed, ("seq", "head"), 0, 0, axis_index_groups=token_groups, tiled=True
    )
    return pl.pallas_call(
        unpack_kernel,
        out_shape=shaped((tokens, GROUP * span), BF16),
        in_specs=[VMEM],
        out_specs=ANY,
        scratch_shapes=[
            pltpu.VMEM((tokens, GROUP * span), BF16),
            pltpu.SemaphoreType.DMA((tokens // 8,)),
        ],
        compiler_params=PARAMS,
        name="unpack",
    )(returned)


def solution(mesh):
    return jax.shard_map(
        functools.partial(local, mesh.shape["seq"], mesh.shape["head"]),
        mesh=mesh,
        in_specs=(
            P(("seq", "head"), None),
            P(("seq", "head"), None),
            P(("seq", "head"), None),
            P("head", "seq"),
            P(),
            P("head"),
        ),
        out_specs=P(("seq", "head"), None),
        check_vma=False,
    )
```

time: 186 us -> 114 us (0.61)
  Pallas kernels: 74.4 us -> 11.9 us
  blocking collectives: 58.8 us -> 15.9 us
  starting transfers between devices: 21 us -> 51.3 us
    pallas_call x6 -> x9, Pallas kernels: 74.4 us -> 11.9 us  [the longest x1 3.44 us: local(): pl.pallas_call(near_kernel, out_shape=(shaped((NH, SEG, DH)), shaped((NH,...]
    all_to_all x1 -> x0, blocking collectives: 39 us -> none  [local(): lax.all_to_all(own, 'seq', 0, 0, axis_index_groups=scan_groups, tiled=True)]
    all_to_all x0 -> x1, starting transfers between devices: none -> 13.7 us  [local(): lax.all_to_all(own.reshape(pieces, 1, PIECE * DH), 'seq', 0, 0, axis_inde...]
    ppermute x1 -> x6, starting transfers between devices: 3.34 us -> 16.8 us  [the longest x3 8.75 us: local(): lax.ppermute(slabs[turn], 'head', [(h, (h // 2 + turn) % XS * 2 + h % 2)...]
    all_to_all x1, waiting for transfers between devices: 12.6 us -> 0.01 us  [local(): lax.all_to_all(prefixes, 'seq', 0, 0, axis_index_groups=scan_groups, tile...]
    ppermute x1 -> x6, waiting for transfers between devices: 16 us -> 26.1 us  [the longest x1 15.2 us: local(): arriving = lax.ppermute(leaving, 'seq', pairs)]
    all_to_all x0 -> x1, waiting for transfers between devices: none -> 3.91 us  [local(): lax.all_to_all(own.reshape(pieces, 1, PIECE * DH), 'seq', 0, 0, axis_inde...]
    all_to_all x1, blocking collectives: 19.7 us -> 15.9 us  [local(): lax.all_to_all(normed, ('seq', 'head'), 0, 0, axis_index_groups=token_gro...]
  transfers between devices with their start and end apart: 3 -> 9, of which waited for: 3 -> 6; matrix products, arithmetic and copies ran while one was open for 0% -> 0% of each run, Pallas kernels for 2% -> 5%
where the time goes in v3:
time: 114 us; the launch traced here: 113 us
  starting transfers between devices  51.3 us (45%)
  waiting for transfers between devices  32.4 us (28%)
  blocking collectives  15.9 us (14%)
  Pallas kernels  11.9 us (10%)
  local copies, waits for them, and re-layouts  1.66 us (1%)
    all_to_all x1, blocking collectives, local(): lax.all_to_all(normed, ('seq', 'head'), 0, 0, axis_index_groups=token_gro...  15.9 us
    ppermute x1, waiting for transfers between devices, local(): arriving = lax.ppermute(leaving, 'seq', pairs)  15.2 us
    all_to_all x1, starting transfers between devices, local(): lax.all_to_all(own.reshape(pieces, 1, PIECE * DH), 'seq', 0, 0, axis_inde...  13.7 us
    all_to_all x1, starting transfers between devices, local(): lax.all_to_all(sent, ('seq', 'head'), 0, 0, axis_index_groups=token_group...  10.5 us
    all_to_all x1, starting transfers between devices, local(): lax.all_to_all(prefixes, 'seq', 0, 0, axis_index_groups=scan_groups, tile...  10.3 us
    ppermute x3, starting transfers between devices, local(): lax.ppermute(slabs[turn], 'head', [(h, (h // 2 + turn) % XS * 2 + h % 2)...  8.75 us
    ppermute x1, waiting for transfers between devices, local(): other_decay = lax.ppermute(log_decay, 'seq', pairs)  6.45 us
    ppermute x3, waiting for transfers between devices, local(): lax.ppermute(slabs[turn], 'head', [(h, (h // 2 + turn) % XS * 2 + h % 2)...  4.47 us
  transfers between devices with their start and end apart: 9, of which 6 were waited for; matrix products, arithmetic and copies ran while one was open for 0% of the time, Pallas kernels for 5%

profile of v3, /device:TPU:1, one launch (start us, length us, event | category | flops | bytes accessed | tf_op | source)
XLA Modules:
  0.0 113.3 jit_solution(1225841357264803296)
XLA Ops:
  0.0 2.2 %pack.1 = bf16[16,2,32,512]{3,2,1,0:T(8,128)(2,1)} custom-call(bf16[32,8192]{1,0:T(8,128)(2,1)} %k_ref.1, bf16[32,8192]{1,0:T(8,128)(2,1)} %v_ref.1), custom_call_target="tpu_custom_call" | custom-call | tf_op jit(solution)/shard_map/pack/pallas_call | solution.py:331
  2.2 0.0 copy-start
  2.2 10.5 %all-to-all-start = ((bf16[16,2,32,512]{3,2,1,0:T(8,128)(2,1)}), bf16[16,2,32,512]{3,2,1,0:T(8,128)(2,1)S(1)}, u32[]{:S(2)}, u32[]{:S(2)}) async-start(bf16[16,2,32,512]{3,2,1,0:T(8,128)(2,1)} %pack.1), calls=%async_computation | async-start | bytes 2097152 | tf_op jit(solution)/shard_map/all_to_all | solution.py:345
  12.6 0.1 pad_add_fusion.place_ref
  12.7 0.0 copy-done
  12.7 0.0 copy-start.1
  12.7 0.8 fold.1
  13.6 2.2 %collective-permute-start = (bf16[4,32,1024]{2,1,0:T(8,128)(2,1)S(1)}, bf16[4,32,1024]{2,1,0:T(8,128)(2,1)S(1)}, u32[]{:S(2)}, u32[]{:S(2)}) collective-permute-start(bf16[4,32,1024]{2,1,0:T(8,128)(2,1)S(1)} %get-tuple-element.28), channel_id=1, source_target_pairs={{0,1},{1,0},{2,3},{3,2},{4,5},{5,4},{6,7},{7,6},{8,9},{9,8},{10,11... | collective-permute-start | bytes 786440 | tf_op jit(solution)/shard_map/ppermute | solution.py:358
  15.7 0.0 copy-done.1
  15.7 3.4 %collective-permute-start.1 = (f32[8,256]{1,0:T(8,128)S(1)}, f32[8,256]{1,0:T(8,128)S(1)}, u32[]{:S(2)}, u32[]{:S(2)}) collective-permute-start(f32[8,256]{1,0:T(8,128)S(1)} %copy-done.1), channel_id=1, source_target_pairs={{0,8},{8,0},{16,24},{24,16},{32,40},{40,32},{48,56},{56,48},{64,72... | collective-permute-start | bytes 24584 | tf_op jit(solution)/shard_map/ppermute | solution.py:330
  19.2 0.0 collective-permute-done.other_ref
  19.2 0.0 copy-start.2
  19.2 0.6 weave.1
  19.8 6.5 %collective-permute-done.1.other_ref = f32[8,256]{1,0:T(8,128)S(1)} collective-permute-done((f32[8,256]{1,0:T(8,128)S(1)}, f32[8,256]{1,0:T(8,128)S(1)}, u32[]{:S(2)}, u32[]{:S(2)}) %collective-permute-start.1) | collective-permute-done | bytes 8224 | tf_op jit(solution)/shard_map/ppermute | solution.py:330
  26.3 2.3 %all-to-all-done.part_ref = bf16[16,2,32,512]{3,2,1,0:T(8,128)(2,1)S(1)} async-done(((bf16[16,2,32,512]{3,2,1,0:T(8,128)(2,1)}), bf16[16,2,32,512]{3,2,1,0:T(8,128)(2,1)S(1)}, u32[]{:S(2)}, u32[]{:S(2)}) %all-to-all-start) | async-done | bytes 1048608 | tf_op jit(solution)/shard_map/all_to_all | solution.py:345
  28.6 0.0 copy-done.2
  28.6 1.9 %state.1 = (f32[544,128]{1,0:T(8,128)}, f32[128,128]{1,0:T(8,128)S(1)}, f32[128,128]{1,0:T(8,128)S(1)}) custom-call(s32[4]{0:T(128)S(1)} %pad_add_fusion.place_ref, s32[32]{0:T(128)S(1)} %copy-done.2, f32[8,256]{1,0:T(8,128)S(1)} %copy-done.1, f32[8,256]{1,0:T(8,128)S(1)} %collective-permute-done.1.other_ref, bf16[16,2,32,512]{3,2,1,0:T(8,128)(2,1)S(1)} %all-to-all-done.part_ref), custom_call_target="tpu_custom_call" | custom-call | tf_op jit(solution)/shard_map/state/pallas_call | solution.py:368
  30.5 13.7 %all-to-all-start.1 = ((f32[32,1,2176]{2,1,0:T(1,128)}), f32[32,1,2176]{2,1,0:T(1,128)S(1)}, u32[]{:S(2)}, u32[]{:S(2)}) async-start(f32[32,1,2176]{2,1,0:T(1,128)} %bitcast.4), calls=%async_computation.1 | async-start | bytes 557056 | tf_op jit(solution)/shard_map/all_to_all | solution.py:385
  44.2 1.9 %collective-permute-start.2 = (bf16[2,32,1024]{2,1,0:T(8,128)(2,1)S(1)}, bf16[2,32,1024]{2,1,0:T(8,128)(2,1)S(1)}, u32[]{:S(2)}, u32[]{:S(2)}) collective-permute-start(bf16[2,32,1024]{2,1,0:T(8,128)(2,1)S(1)} %get-tuple-element.36), channel_id=1, source_target_pairs={{0,2},{1,3},{2,4},{3,5},{4,6},{5,7},{6,0},{7,1},{8,10},{9,11},{10,... | collective-permute-start | bytes 393224 | tf_op jit(solution)/shard_map/ppermute | solution.py:389
  46.1 4.9 %collective-permute-start.3 = (bf16[2,32,1024]{2,1,0:T(8,128)(2,1)S(1)}, bf16[2,32,1024]{2,1,0:T(8,128)(2,1)S(1)}, u32[]{:S(2)}, u32[]{:S(2)}) collective-permute-start(bf16[2,32,1024]{2,1,0:T(8,128)(2,1)S(1)} %get-tuple-element.37), channel_id=1, source_target_pairs={{0,4},{1,5},{2,6},{3,7},{4,0},{5,1},{6,2},{7,3},{8,12},{9,13},{10,... | collective-permute-start | bytes 393224 | tf_op jit(solution)/shard_map/ppermute | solution.py:389
  51.0 1.9 %collective-permute-start.4 = (bf16[2,32,1024]{2,1,0:T(8,128)(2,1)S(1)}, bf16[2,32,1024]{2,1,0:T(8,128)(2,1)S(1)}, u32[]{:S(2)}, u32[]{:S(2)}) collective-permute-start(bf16[2,32,1024]{2,1,0:T(8,128)(2,1)S(1)} %get-tuple-element.38), channel_id=1, source_target_pairs={{0,6},{1,7},{2,0},{3,1},{4,2},{5,3},{6,4},{7,5},{8,14},{9,15},{10,... | collective-permute-start | bytes 393224 | tf_op jit(solution)/shard_map/ppermute | solution.py:389
  53.0 0.0 collective-permute-done.2.refs_1_
  53.0 2.1 %collective-permute-done.3.refs_2_ = bf16[2,32,1024]{2,1,0:T(8,128)(2,1)S(1)} collective-permute-done((bf16[2,32,1024]{2,1,0:T(8,128)(2,1)S(1)}, bf16[2,32,1024]{2,1,0:T(8,128)(2,1)S(1)}, u32[]{:S(2)}, u32[]{:S(2)}) %collective-permute-start.3) | collective-permute-done | bytes 131104 | tf_op jit(solution)/shard_map/ppermute | solution.py:389
  55.1 2.4 %collective-permute-done.4.refs_3_ = bf16[2,32,1024]{2,1,0:T(8,128)(2,1)S(1)} collective-permute-done((bf16[2,32,1024]{2,1,0:T(8,128)(2,1)S(1)}, bf16[2,32,1024]{2,1,0:T(8,128)(2,1)S(1)}, u32[]{:S(2)}, u32[]{:S(2)}) %collective-permute-start.4) | collective-permute-done | bytes 131104 | tf_op jit(solution)/shard_map/ppermute | solution.py:389
  57.4 0.6 regroup.1
  58.0 0.0 copy-start.3
  58.0 0.7 copy-done.3
  58.7 3.9 %all-to-all-done.1 = f32[32,1,2176]{2,1,0:T(1,128)S(1)} async-done(((f32[32,1,2176]{2,1,0:T(1,128)}), f32[32,1,2176]{2,1,0:T(1,128)S(1)}, u32[]{:S(2)}, u32[]{:S(2)}) %all-to-all-start.1) | async-done | bytes 278560 | tf_op jit(solution)/shard_map/all_to_all | solution.py:385
  62.6 0.7 scan.1
  63.4 10.3 %all-to-all-start.2 = ((f32[32,16,128]{2,1,0:T(8,128)}), f32[32,16,128]{2,1,0:T(8,128)S(1)}, u32[]{:S(2)}, u32[]{:S(2)}) async-start(f32[32,16,128]{2,1,0:T(8,128)} %scan.1), calls=%async_computation.2 | async-start | bytes 524288 | tf_op jit(solution)/shard_map/all_to_all | solution.py:417
  73.7 0.0 copy-start.5
  73.7 2.4 %collective-permute-start.5 = (bf16[8,32,512]{2,1,0:T(8,128)(2,1)S(1)}, bf16[8,32,512]{2,1,0:T(8,128)(2,1)S(1)}, u32[]{:S(2)}, u32[]{:S(2)}) collective-permute-start(bf16[8,32,512]{2,1,0:T(8,128)(2,1)S(1)} %get-tuple-element.42), channel_id=1, source_target_pairs={{0,8},{8,0},{16,24},{24,16},{32,40},{40,32},{48,56},{56,48},{64,72... | collective-permute-start | bytes 786440 | tf_op jit(solution)/shard_map/ppermute | solution.py:420
  76.1 15.2 %collective-permute-done.5.other_ref = bf16[8,32,512]{2,1,0:T(8,128)(2,1)S(1)} collective-permute-done((bf16[8,32,512]{2,1,0:T(8,128)(2,1)S(1)}, bf16[8,32,512]{2,1,0:T(8,128)(2,1)S(1)}, u32[]{:S(2)}, u32[]{:S(2)}) %collective-permute-start.5) | collective-permute-done | bytes 262176 | tf_op jit(solution)/shard_map/ppermute | solution.py:420
  91.4 0.0 copy-done.5
  91.4 0.0 copy-start.4
  91.4 0.9 copy-done.4
  92.3 3.4 %near.1 = (f32[4,512,128]{2,1,0:T(8,128)S(1)}, bf16[4,512,256]{2,1,0:T(8,128)(2,1)S(1)}, f32[8,128]{1,0:T(8,128)S(1)}) custom-call(s32[4]{0:T(128)S(1)} %pad_add_fusion.place_ref, bf16[8,32,512]{2,1,0:T(8,128)(2,1)S(1)} %copy-done.4, bf16[8,32,512]{2,1,0:T(8,128)(2,1)S(1)} %collective-permute-done.5.other_ref, ...), custom_call_target="tpu_custom_call" | custom-call | flops 500000000 | bytes 4000000 | tf_op jit(solution)/shard_map/near/pallas_call | solution.py:421
  95.8 0.0 all-to-all-done.2
  95.8 0.8 close.1
  96.6 15.9 %all_to_all.20.in_ref = bf16[16,32,512]{2,1,0:T(8,128)(2,1)S(1)} all-to-all(bf16[16,32,512]{2,1,0:T(8,128)(2,1)S(1)} %close.1), channel_id=1, replica_groups={{0,1,2,3,4,5,6,7,8,9,10,11,12,13,14,15},{16,17,18,19,20,21,22,23,24,25,..., dimensions={0} | all-to-all | bytes 1048576 | tf_op jit(solution)/shard_map/all_to_all | solution.py:442
  112.5 0.8 unpack.1
Async XLA Ops:
  2.2 10.6 %copy-start = (bf16[32,8192]{1,0:T(8,128)(2,1)S(1)}, bf16[32,8192]{1,0:T(8,128)(2,1)}, u32[]{:S(2)}) copy-start(bf16[32,8192]{1,0:T(8,128)(2,1)} %q_ref.1) | copy-start | bytes 1572868
  2.2 26.4 %all-to-all-start = ((bf16[16,2,32,512]{3,2,1,0:T(8,128)(2,1)}), bf16[16,2,32,512]{3,2,1,0:T(8,128)(2,1)S(1)}, u32[]{:S(2)}, u32[]{:S(2)}) async-start(bf16[16,2,32,512]{3,2,1,0:T(8,128)(2,1)} %pack.1), calls=%async_computation | async-start | bytes 2097152 | tf_op jit(solution)/shard_map/all_to_all | solution.py:345
  12.7 3.0 %copy-start.1 = (f32[8,256]{1,0:T(8,128)S(1)}, f32[8,256]{1,0:T(8,128)}, u32[]{:S(2)}) copy-start(f32[8,256]{1,0:T(8,128)} %own_ref.1) | copy-start | bytes 24580
  13.6 5.6 %collective-permute-start = (bf16[4,32,1024]{2,1,0:T(8,128)(2,1)S(1)}, bf16[4,32,1024]{2,1,0:T(8,128)(2,1)S(1)}, u32[]{:S(2)}, u32[]{:S(2)}) collective-permute-start(bf16[4,32,1024]{2,1,0:T(8,128)(2,1)S(1)} %get-tuple-element.28), channel_id=1, source_target_pairs={{0,1},{1,0},{2,3},{3,2},{4,5},{5,4},{6,7},{7,6},{8,9},{9,8},{10,11... | collective-permute-start | bytes 786440 | tf_op jit(solution)/shard_map/ppermute | solution.py:358
  15.7 10.5 %collective-permute-start.1 = (f32[8,256]{1,0:T(8,128)S(1)}, f32[8,256]{1,0:T(8,128)S(1)}, u32[]{:S(2)}, u32[]{:S(2)}) collective-permute-start(f32[8,256]{1,0:T(8,128)S(1)} %copy-done.1), channel_id=1, source_target_pairs={{0,8},{8,0},{16,24},{24,16},{32,40},{40,32},{48,56},{56,48},{64,72... | collective-permute-start | bytes 24584 | tf_op jit(solution)/shard_map/ppermute | solution.py:330
  19.2 9.4 %copy-start.2 = (s32[32]{0:T(128)S(1)}, s32[32]{0:T(128)}, u32[]{:S(2)}) copy-start(s32[32]{0:T(128)} %lengths_ref.1) | copy-start | bytes 388
  30.5 32.2 %all-to-all-start.1 = ((f32[32,1,2176]{2,1,0:T(1,128)}), f32[32,1,2176]{2,1,0:T(1,128)S(1)}, u32[]{:S(2)}, u32[]{:S(2)}) async-start(f32[32,1,2176]{2,1,0:T(1,128)} %bitcast.4), calls=%async_computation.1 | async-start | bytes 557056 | tf_op jit(solution)/shard_map/all_to_all | solution.py:385
  44.2 8.8 %collective-permute-start.2 = (bf16[2,32,1024]{2,1,0:T(8,128)(2,1)S(1)}, bf16[2,32,1024]{2,1,0:T(8,128)(2,1)S(1)}, u32[]{:S(2)}, u32[]{:S(2)}) collective-permute-start(bf16[2,32,1024]{2,1,0:T(8,128)(2,1)S(1)} %get-tuple-element.36), channel_id=1, source_target_pairs={{0,2},{1,3},{2,4},{3,5},{4,6},{5,7},{6,0},{7,1},{8,10},{9,11},{10,... | collective-permute-start | bytes 393224 | tf_op jit(solution)/shard_map/ppermute | solution.py:389
  46.1 9.0 %collective-permute-start.3 = (bf16[2,32,1024]{2,1,0:T(8,128)(2,1)S(1)}, bf16[2,32,1024]{2,1,0:T(8,128)(2,1)S(1)}, u32[]{:S(2)}, u32[]{:S(2)}) collective-permute-start(bf16[2,32,1024]{2,1,0:T(8,128)(2,1)S(1)} %get-tuple-element.37), channel_id=1, source_target_pairs={{0,4},{1,5},{2,6},{3,7},{4,0},{5,1},{6,2},{7,3},{8,12},{9,13},{10,... | collective-permute-start | bytes 393224 | tf_op jit(solution)/shard_map/ppermute | solution.py:389
  51.0 6.4 %collective-permute-start.4 = (bf16[2,32,1024]{2,1,0:T(8,128)(2,1)S(1)}, bf16[2,32,1024]{2,1,0:T(8,128)(2,1)S(1)}, u32[]{:S(2)}, u32[]{:S(2)}) collective-permute-start(bf16[2,32,1024]{2,1,0:T(8,128)(2,1)S(1)} %get-tuple-element.38), channel_id=1, source_target_pairs={{0,6},{1,7},{2,0},{3,1},{4,2},{5,3},{6,4},{7,5},{8,14},{9,15},{10,... | collective-permute-start | bytes 393224 | tf_op jit(solution)/shard_map/ppermute | solution.py:389
  58.0 0.7 copy-start.3
  63.4 32.4 %all-to-all-start.2 = ((f32[32,16,128]{2,1,0:T(8,128)}), f32[32,16,128]{2,1,0:T(8,128)S(1)}, u32[]{:S(2)}, u32[]{:S(2)}) async-start(f32[32,16,128]{2,1,0:T(8,128)} %scan.1), calls=%async_computation.2 | async-start | bytes 524288 | tf_op jit(solution)/shard_map/all_to_all | solution.py:417
  73.7 17.6 %copy-start.5 = (f32[1024]{0:T(1024)S(1)}, f32[1024]{0:T(1024)}, u32[]{:S(2)}) copy-start(f32[1024]{0:T(1024)} %param.11) | copy-start | bytes 12292
  73.7 17.6 %collective-permute-start.5 = (bf16[8,32,512]{2,1,0:T(8,128)(2,1)S(1)}, bf16[8,32,512]{2,1,0:T(8,128)(2,1)S(1)}, u32[]{:S(2)}, u32[]{:S(2)}) collective-permute-start(bf16[8,32,512]{2,1,0:T(8,128)(2,1)S(1)} %get-tuple-element.42), channel_id=1, source_target_pairs={{0,8},{8,0},{16,24},{24,16},{32,40},{40,32},{48,56},{56,48},{64,72... | collective-permute-start | bytes 786440 | tf_op jit(solution)/shard_map/ppermute | solution.py:420
  91.4 1.0 copy-start.4

commit v4 on v3

--- a/solution.py
+++ b/solution.py
@@ -15,11 +15,11 @@
 PAIR = 2
 NH = 4
 SEG = CH * NC
+XS = 4
 GROUP = 16
-XS = 4
 ROWS = 16
 PIECE = ROWS + 1
-VMEM_LIMIT = 16 * 1024 * 1024
+VMEM_LIMIT = 48 * 1024 * 1024
 
 
 def split2(x):
@@ -79,44 +79,6 @@
             copy.wait()
 
 
-def fold_kernel(place_ref, q_ref, keep_ref, send_ref, sems):
-    across, core = place_ref[2], place_ref[3]
-    width = 2 * NH * DH
-    copies = []
-    for turn in range(XS):
-        base = 2 * lax.rem(across + turn, XS)
-        for which, ref in enumerate((keep_ref, send_ref)):
-            goal = base + (core if which == 0 else 1 - core)
-            columns = pl.ds(pl.multiple_of(goal * width, width), width)
-            copies.append(
-                pltpu.make_async_copy(q_ref.at[:, columns], ref.at[turn], sems.at[turn, which])
-            )
-    for copy in copies:
-        copy.start()
-    for copy in copies:
-        copy.wait()
-
-
-def weave_kernel(place_ref, keep_ref, other_ref, *slab_refs):
-    core = place_ref[3]
-    for turn, slab_ref in enumerate(slab_refs):
-        slab_ref[core] = keep_ref[turn]
-        slab_ref[1 - core] = other_ref[turn]
-
-
-def regroup_kernel(place_ref, *refs):
-    half, across = place_ref[1], place_ref[2]
-    slab_refs, (keep_ref, send_ref) = refs[:XS], refs[XS:]
-    span = NH * DH
-    mine = pl.ds(pl.multiple_of(half * span, span), span)
-    theirs = pl.ds(pl.multiple_of((1 - half) * span, span), span)
-    for turn, slab_ref in enumerate(slab_refs):
-        origin = lax.rem(across + XS - turn, XS)
-        for core in range(2):
-            keep_ref[2 * origin + core] = slab_ref[core, :, mine]
-            send_ref[2 * origin + core] = slab_ref[core, :, theirs]
-
-
 def unpack_kernel(in_ref, out_ref, ready, sems):
     tokens = in_ref.shape[1]
     span = NH * DH
@@ -134,11 +96,45 @@
         copy.wait()
 
 
+def slab_kernel(place_ref, q_ref, *refs):
+    outs, sems = refs[:XS], refs[XS]
+    width = GROUP // XS * NH * DH
+    copies = []
+    for turn in range(XS):
+        goal = lax.rem(place_ref[2] + turn, XS)
+        columns = pl.ds(pl.multiple_of(goal * width, width), width)
+        copies.append(pltpu.make_async_copy(q_ref.at[:, columns], outs[turn], sems.at[turn]))
+    for copy in copies:
+        copy.start()
+    for copy in copies:
+        copy.wait()
+
+
+def regroup_kernel(place_ref, *refs):
+    half, across, core = place_ref[1], place_ref[2], place_ref[3]
+    span = NH * DH
+    for far, out_ref in enumerate(refs[XS:]):
+        goal = 2 * lax.rem(core + far % 2, 2) + lax.rem(half + far // 2, 2)
+        columns = pl.ds(pl.multiple_of(goal * span, span), span)
+        for turn, in_ref in enumerate(refs[:XS]):
+            origin = lax.rem(across + XS - turn, XS)
+            out_ref[origin] = in_ref[:, columns]
+
+
+def settle_kernel(place_ref, *refs):
+    half, core = place_ref[1], place_ref[3]
+    out_ref = refs[-1]
+    for far, in_ref in enumerate(refs[:-1]):
+        start = 8 * lax.rem(half + far // 2, 2) + lax.rem(core + far % 2, 2)
+        for origin in range(XS):
+            out_ref[start + 2 * origin] = in_ref[origin]
+
+
 def pick_heads(tile, half):
     return jnp.where(half == 0, tile, pltpu.roll(tile, 4, axis=0))
 
 
-def state_kernel(place_ref, lengths_ref, own_ref, other_ref, part_ref, out_ref, rows_ref, cols_ref, send_ref, sems):
+def state_kernel(place_ref, lengths_ref, own_ref, other_ref, part_ref, gain_in_ref, out_ref, rows_ref, cols_ref, gain_ref, send_ref, sems):
     segment, half = place_ref[0], place_ref[1]
     own, other = own_ref[...], other_ref[...]
     first = jnp.where(half == 0, own, other)
@@ -199,6 +195,7 @@
     cols_ref[...] = table.T
 
     full_tails = [t * a for t, a in zip(tails, after)]
+    gain_ref[...] = pick_heads(gain_in_ref[...], half)
     copies = []
     for head in range(NH):
         at = slice(head * DH, (head + 1) * DH)
@@ -219,11 +216,7 @@
         copy.wait()
 
 
-def near_kernel(
-    place_ref, own_ref, other_ref, part_ref, rows_ref, cols_ref, gain_in_ref, near_ref, scaled_ref, gain_ref
-):
-    half = place_ref[1]
-    gain_ref[...] = pick_heads(gain_in_ref[...], half)
+def near_kernel(q_ref, part_ref, rows_ref, cols_ref, near_ref, scaled_ref):
     order = lax.broadcasted_iota(jnp.int32, (CH, CH), 0) >= lax.broadcasted_iota(
         jnp.int32, (CH, CH), 1
     )
@@ -239,10 +232,7 @@
         for c in range(NC):
             part = slice(4 * c, 4 * c + 4)
             row = 8 * c + head
-            blocks = slice(4 * (c % 2), 4 * (c % 2) + 4)
-            query = jnp.where(
-                half == c // 2, own_ref[blocks, :, at], other_ref[blocks, :, at]
-            ).reshape(CH, DH)
+            query = q_ref[part, :, at].reshape(CH, DH)
             key_part = part_ref[part, 0, :, at].reshape(CH, DH)
             value_part = part_ref[part, 1, :, at].reshape(CH, DH)
             keys_across = key_part.T
@@ -316,26 +306,25 @@
 
 def local(seq_size, head_size, queries, keys, values, log_decay, doc_lengths, gain):
     tokens = queries.shape[0]
-    span = NH * DH
     segments = seq_size // PAIR
     pieces = NH * DH // ROWS
-    seq, head = lax.axis_index("seq"), lax.axis_index("head")
+    seq = lax.axis_index("seq")
+    head = lax.axis_index("head")
     place = jnp.stack([seq // PAIR, seq % PAIR, head // 2, head % 2]).astype(jnp.int32)
     token_groups = [
         [g * GROUP + i for i in range(GROUP)] for g in range(seq_size * head_size // GROUP)
     ]
     scan_groups = [[g * PAIR + i for g in range(segments)] for i in range(PAIR)]
-    pairs = [(s, s ^ 1) for s in range(seq_size)]
-
-    other_decay = lax.ppermute(log_decay, "seq", pairs)
+
+    other_decay = lax.ppermute(log_decay, "seq", [(s, s ^ 1) for s in range(seq_size)])
     sent = pl.pallas_call(
         pack_kernel,
-        out_shape=shaped((GROUP, 2, tokens, span), BF16),
+        out_shape=shaped((GROUP, 2, tokens, NH * DH), BF16),
         in_specs=[ANY] * 2,
         out_specs=ANY,
         scratch_shapes=[
-            pltpu.VMEM((2, tokens, GROUP * span), BF16),
-            pltpu.VMEM((GROUP, 2, tokens, span), BF16),
+            pltpu.VMEM((2, tokens, GROUP * NH * DH), BF16),
+            pltpu.VMEM((GROUP, 2, tokens, NH * DH), BF16),
             pltpu.SemaphoreType.DMA((4, 2)),
             pltpu.SemaphoreType.DMA((4, 2)),
         ],
@@ -345,46 +334,34 @@
     parts = lax.all_to_all(
         sent, ("seq", "head"), 0, 0, axis_index_groups=token_groups, tiled=True
     )
-
-    kept, folded = pl.pallas_call(
-        fold_kernel,
-        out_shape=[shaped((XS, tokens, 2 * span), BF16)] * 2,
-        in_specs=[SMEM, ANY],
-        out_specs=[VMEM] * 2,
-        scratch_shapes=[pltpu.SemaphoreType.DMA((XS, 2))],
-        compiler_params=PARAMS,
-        name="fold",
-    )(place, queries)
-    unfolded = lax.ppermute(folded, "head", [(h, h ^ 1) for h in range(head_size)])
-    slabs = pl.pallas_call(
-        weave_kernel,
-        out_shape=[shaped((2, tokens, 2 * span), BF16)] * XS,
-        in_specs=[SMEM, VMEM, VMEM],
-        out_specs=[VMEM] * XS,
-        compiler_params=PARAMS,
-        name="weave",
-    )(place, kept, unfolded)
-
-    own, rows, cols = pl.pallas_call(
+    own, rows, cols, gains = pl.pallas_call(
         state_kernel,
         out_shape=(
             shaped((pieces * PIECE, DH)),
             shaped((128, CH)),
             shaped((CH, 128)),
+            shaped((8, DH)),
         ),
-        in_specs=[SMEM, SMEM, VMEM, VMEM, VMEM],
-        out_specs=(ANY, VMEM, VMEM),
+        in_specs=[SMEM, SMEM, VMEM, VMEM, VMEM, VMEM],
+        out_specs=(ANY, VMEM, VMEM, VMEM),
         scratch_shapes=[
             pltpu.VMEM((pieces * PIECE, DH), F32),
             pltpu.SemaphoreType.DMA((NH,)),
         ],
         compiler_params=PARAMS,
         name="state",
-    )(place, doc_lengths, log_decay, other_decay, parts)
+    )(place, doc_lengths, log_decay, other_decay, parts, gain.reshape(8, DH))
+    span = GROUP // XS * NH * DH
+    slabs = pl.pallas_call(
+        slab_kernel,
+        out_shape=[shaped((tokens, span), BF16)] * XS,
+        in_specs=[SMEM, ANY],
+        out_specs=[VMEM] * XS,
+        scratch_shapes=[pltpu.SemaphoreType.DMA((XS,))],
+        compiler_params=PARAMS,
+        name="slab",
+    )(place, queries)
     slabs, own = lax.optimization_barrier((slabs, own))
-    gathered = lax.all_to_all(
-        own.reshape(pieces, 1, PIECE * DH), "seq", 0, 0, axis_index_groups=scan_groups, tiled=True
-    ).reshape(pieces * PIECE, DH)
     turned = [slabs[0]] + [
         lax.ppermute(
             slabs[turn],
@@ -393,15 +370,18 @@
         )
         for turn in range(1, XS)
     ]
-    kept_queries, leaving = pl.pallas_call(
+    grouped = pl.pallas_call(
         regroup_kernel,
-        out_shape=[shaped((2 * XS, tokens, span), BF16)] * 2,
+        out_shape=[shaped((XS, tokens, NH * DH), BF16)] * 4,
         in_specs=[SMEM] + [VMEM] * XS,
-        out_specs=[VMEM] * 2,
+        out_specs=[VMEM] * 4,
         compiler_params=PARAMS,
         name="regroup",
     )(place, *turned)
-    gathered, kept_queries, leaving = lax.optimization_barrier((gathered, kept_queries, leaving))
+    gathered = lax.all_to_all(
+        own.reshape(pieces, 1, PIECE * DH), "seq", 0, 0, axis_index_groups=scan_groups, tiled=True
+    ).reshape(pieces * PIECE, DH)
+    gathered, grouped = lax.optimization_barrier((gathered, grouped))
     prefixes = pl.pallas_call(
         scan_kernel,
         out_shape=shaped((segments, ROWS, DH)),
@@ -414,26 +394,41 @@
         compiler_params=PARAMS,
         name="scan",
     )(gathered)
+    swapped = [grouped[0]] + [
+        lax.ppermute(
+            grouped[far],
+            ("seq", "head"),
+            [
+                (s * head_size + h, (s ^ (far // 2)) * head_size + (h ^ (far % 2)))
+                for s in range(seq_size)
+                for h in range(head_size)
+            ],
+        )
+        for far in range(1, 4)
+    ]
+    query_parts = pl.pallas_call(
+        settle_kernel,
+        out_shape=shaped((GROUP, tokens, NH * DH), BF16),
+        in_specs=[SMEM] + [VMEM] * 4,
+        out_specs=VMEM,
+        compiler_params=PARAMS,
+        name="settle",
+    )(place, *swapped)
+    near, scaled = pl.pallas_call(
+        near_kernel,
+        out_shape=(shaped((NH, SEG, DH)), shaped((NH, SEG, 2 * DH), BF16)),
+        in_specs=[VMEM, VMEM, VMEM, VMEM],
+        out_specs=(VMEM, VMEM),
+        compiler_params=PARAMS,
+        cost_estimate=pl.CostEstimate(flops=500000000, transcendentals=300000, bytes_accessed=4000000),
+        name="near",
+    )(query_parts, parts, rows, cols)
     incoming = lax.all_to_all(
         prefixes, "seq", 0, 0, axis_index_groups=scan_groups, tiled=True
     ).reshape(NH, DH, DH)
-    arriving = lax.ppermute(leaving, "seq", pairs)
-    near, scaled, gains = pl.pallas_call(
-        near_kernel,
-        out_shape=(
-            shaped((NH, SEG, DH)),
-            shaped((NH, SEG, 2 * DH), BF16),
-            shaped((8, DH)),
-        ),
-        in_specs=[SMEM] + [VMEM] * 6,
-        out_specs=(VMEM, VMEM, VMEM),
-        compiler_params=PARAMS,
-        cost_estimate=pl.CostEstimate(flops=500000000, transcendentals=300000, bytes_accessed=4000000),
-        name="near",
-    )(place, kept_queries, arriving, parts, rows, cols, gain.reshape(8, DH))
     normed = pl.pallas_call(
         close_kernel,
-        out_shape=shaped((GROUP, tokens, span), BF16),
+        out_shape=shaped((GROUP, tokens, NH * DH), BF16),
         in_specs=[VMEM] * 4,
         out_specs=VMEM,
         compiler_params=PARAMS,
@@ -444,11 +439,11 @@
     )
     return pl.pallas_call(
         unpack_kernel,
-        out_shape=shaped((tokens, GROUP * span), BF16),
+        out_shape=shaped((tokens, GROUP * NH * DH), BF16),
         in_specs=[VMEM],
         out_specs=ANY,
         scratch_shapes=[
-            pltpu.VMEM((tokens, GROUP * span), BF16),
+            pltpu.VMEM((tokens, GROUP * NH * DH), BF16),
             pltpu.SemaphoreType.DMA((tokens // 8,)),
         ],
         compiler_params=PARAMS,

time: 114 us -> 112 us (0.982)
  starting transfers between devices: 51.3 us -> 55.3 us
  waiting for transfers between devices: 32.4 us -> 30.2 us
  local copies, waits for them, and re-layouts: 1.66 us -> 0.02 us
  blocking collectives: 15.9 us -> 14.6 us
    ppermute x3 -> x4, starting transfers between devices: 8.01 us -> 12.7 us  [the longest x3 9.38 us: local(): lax.ppermute(grouped[far], ('seq', 'head'), [(s * head_size + h, (s ^ far...]
    ppermute x3 -> x4, waiting for transfers between devices: 21.7 us -> 18.9 us  [the longest x3 9.51 us: local(): lax.ppermute(grouped[far], ('seq', 'head'), [(s * head_size + h, (s ^ far...]
    unnamed x12 -> x8, local copies, waits for them, and re-layouts: 1.66 us -> 0.02 us
    all_to_all x1, blocking collectives: 15.9 us -> 14.6 us  [local(): lax.all_to_all(normed, ('seq', 'head'), 0, 0, axis_index_groups=token_gro...]
  transfers between devices with their start and end apart: 9 -> 10, of which waited for: 6 -> 7; matrix products, arithmetic and copies ran while one was open for 0% -> 0% of each run, Pallas kernels for 5% -> 4%
where the time goes in v4:
time: 112 us
  starting transfers between devices  55.3 us (49%)
  waiting for transfers between devices  30.2 us (27%)
  blocking collectives  14.6 us (13%)
  Pallas kernels  11.3 us (10%)
    all_to_all x1, blocking collectives, local(): lax.all_to_all(normed, ('seq', 'head'), 0, 0, axis_index_groups=token_gro...  14.6 us
    all_to_all x1, starting transfers between devices, local(): lax.all_to_all(own.reshape(pieces, 1, PIECE * DH), 'seq', 0, 0, axis_inde...  13.7 us
    all_to_all x1, starting transfers between devices, local(): lax.all_to_all(sent, ('seq', 'head'), 0, 0, axis_index_groups=token_group...  10.5 us
    all_to_all x1, starting transfers between devices, local(): lax.all_to_all(prefixes, 'seq', 0, 0, axis_index_groups=scan_groups, tile...  9.65 us
    ppermute x3, waiting for transfers between devices, local(): lax.ppermute(grouped[far], ('seq', 'head'), [(s * head_size + h, (s ^ far...  9.51 us
    ppermute x3, starting transfers between devices, local(): lax.ppermute(grouped[far], ('seq', 'head'), [(s * head_size + h, (s ^ far...  9.38 us
    ppermute x1, waiting for transfers between devices, local(): lax.ppermute(log_decay, 'seq', [(s, s ^ 1) for s in range(seq_size)])  9.35 us
    ppermute x3, starting transfers between devices, local(): lax.ppermute(slabs[turn], 'head', [(h, (h // 2 + turn) % XS * 2 + h % 2)...  8.75 us
  transfers between devices with their start and end apart: 10, of which 7 were waited for; matrix products, arithmetic and copies ran while one was open for 0% of the time, Pallas kernels for 4%

profile of v4, /device:TPU:1, one launch (start us, length us, event | category | flops | bytes accessed | tf_op | source)
XLA Modules:
  0.0 111.7 jit_solution(10823127465925212782)
XLA Ops:
  0.0 2.1 %pack.1 = bf16[16,2,32,512]{3,2,1,0:T(8,128)(2,1)} custom-call(bf16[32,8192]{1,0:T(8,128)(2,1)} %k_ref.1, bf16[32,8192]{1,0:T(8,128)(2,1)} %v_ref.1), custom_call_target="tpu_custom_call" | custom-call | tf_op jit(solution)/shard_map/pack/pallas_call | solution.py:320
  2.2 0.0 copy-start.1
  2.2 0.0 copy-start
  2.2 10.5 %all-to-all-start = ((bf16[16,2,32,512]{3,2,1,0:T(8,128)(2,1)}), bf16[16,2,32,512]{3,2,1,0:T(8,128)(2,1)S(1)}, u32[]{:S(2)}, u32[]{:S(2)}) async-start(bf16[16,2,32,512]{3,2,1,0:T(8,128)(2,1)} %pack.1), calls=%async_computation | async-start | bytes 2097152 | tf_op jit(solution)/shard_map/all_to_all | solution.py:334
  12.6 0.0 copy-done.1
  12.6 3.3 %collective-permute-start = (f32[8,256]{1,0:T(8,128)S(1)}, f32[8,256]{1,0:T(8,128)S(1)}, u32[]{:S(2)}, u32[]{:S(2)}) collective-permute-start(f32[8,256]{1,0:T(8,128)S(1)} %copy-done.1), channel_id=1, source_target_pairs={{0,8},{8,0},{16,24},{24,16},{32,40},{40,32},{48,56},{56,48},{64,72... | collective-permute-start | bytes 24584 | tf_op jit(solution)/shard_map/ppermute | solution.py:319
  16.0 0.1 pad_add_fusion.place_ref
  16.1 0.0 copy-done
  16.1 0.0 copy-start.2
  16.1 0.8 slab.1
  16.9 0.0 copy-start.3
  16.9 9.3 %collective-permute-done.other_ref = f32[8,256]{1,0:T(8,128)S(1)} collective-permute-done((f32[8,256]{1,0:T(8,128)S(1)}, f32[8,256]{1,0:T(8,128)S(1)}, u32[]{:S(2)}, u32[]{:S(2)}) %collective-permute-start) | collective-permute-done | bytes 8224 | tf_op jit(solution)/shard_map/ppermute | solution.py:319
  26.2 2.3 %all-to-all-done.part_ref = bf16[16,2,32,512]{3,2,1,0:T(8,128)(2,1)S(1)} async-done(((bf16[16,2,32,512]{3,2,1,0:T(8,128)(2,1)}), bf16[16,2,32,512]{3,2,1,0:T(8,128)(2,1)S(1)}, u32[]{:S(2)}, u32[]{:S(2)}) %all-to-all-start) | async-done | bytes 1048608 | tf_op jit(solution)/shard_map/all_to_all | solution.py:334
  28.5 0.0 copy-done.2
  28.5 0.0 copy-done.3
  28.6 1.9 %state.1 = (f32[544,128]{1,0:T(8,128)}, f32[128,128]{1,0:T(8,128)S(1)}, f32[128,128]{1,0:T(8,128)S(1)}, f32[8,128]{1,0:T(8,128)S(1)}) custom-call(s32[4]{0:T(128)S(1)} %pad_add_fusion.place_ref, s32[32]{0:T(128)S(1)} %copy-done.3, f32[8,256]{1,0:T(8,128)S(1)} %copy-done.1, f32[8,256]{1,0:T(8,128)S(1)} %collective-permute-done.other_ref, ...), custom_call_target="tpu_custom_call" | custom-call | tf_op jit(solution)/shard_map/state/pallas_call | solution.py:337
  30.5 13.7 %all-to-all-start.1 = ((f32[32,1,2176]{2,1,0:T(1,128)}), f32[32,1,2176]{2,1,0:T(1,128)S(1)}, u32[]{:S(2)}, u32[]{:S(2)}) async-start(f32[32,1,2176]{2,1,0:T(1,128)} %bitcast.5), calls=%async_computation.1 | async-start | bytes 557056 | tf_op jit(solution)/shard_map/all_to_all | solution.py:381
  44.2 1.9 %collective-permute-start.1 = (bf16[32,2048]{1,0:T(8,128)(2,1)S(1)}, bf16[32,2048]{1,0:T(8,128)(2,1)S(1)}, u32[]{:S(2)}, u32[]{:S(2)}) collective-permute-start(bf16[32,2048]{1,0:T(8,128)(2,1)S(1)} %get-tuple-element.36), channel_id=1, source_target_pairs={{0,2},{1,3},{2,4},{3,5},{4,6},{5,7},{6,0},{7,1},{8,10},{9,11},{10,... | collective-permute-start | bytes 393224 | tf_op jit(solution)/shard_map/ppermute | solution.py:366
  46.1 4.9 %collective-permute-start.2 = (bf16[32,2048]{1,0:T(8,128)(2,1)S(1)}, bf16[32,2048]{1,0:T(8,128)(2,1)S(1)}, u32[]{:S(2)}, u32[]{:S(2)}) collective-permute-start(bf16[32,2048]{1,0:T(8,128)(2,1)S(1)} %get-tuple-element.37), channel_id=1, source_target_pairs={{0,4},{1,5},{2,6},{3,7},{4,0},{5,1},{6,2},{7,3},{8,12},{9,13},{10,... | collective-permute-start | bytes 393224 | tf_op jit(solution)/shard_map/ppermute | solution.py:366
  51.0 1.9 %collective-permute-start.3 = (bf16[32,2048]{1,0:T(8,128)(2,1)S(1)}, bf16[32,2048]{1,0:T(8,128)(2,1)S(1)}, u32[]{:S(2)}, u32[]{:S(2)}) collective-permute-start(bf16[32,2048]{1,0:T(8,128)(2,1)S(1)} %get-tuple-element.38), channel_id=1, source_target_pairs={{0,6},{1,7},{2,0},{3,1},{4,2},{5,3},{6,4},{7,5},{8,14},{9,15},{10,... | collective-permute-start | bytes 393224 | tf_op jit(solution)/shard_map/ppermute | solution.py:366
  53.0 0.0 collective-permute-done.1.refs_1_
  53.0 2.1 %collective-permute-done.2.refs_2_ = bf16[32,2048]{1,0:T(8,128)(2,1)S(1)} collective-permute-done((bf16[32,2048]{1,0:T(8,128)(2,1)S(1)}, bf16[32,2048]{1,0:T(8,128)(2,1)S(1)}, u32[]{:S(2)}, u32[]{:S(2)}) %collective-permute-start.2) | collective-permute-done | bytes 131104 | tf_op jit(solution)/shard_map/ppermute | solution.py:366
  55.1 2.4 %collective-permute-done.3.refs_3_ = bf16[32,2048]{1,0:T(8,128)(2,1)S(1)} collective-permute-done((bf16[32,2048]{1,0:T(8,128)(2,1)S(1)}, bf16[32,2048]{1,0:T(8,128)(2,1)S(1)}, u32[]{:S(2)}, u32[]{:S(2)}) %collective-permute-start.3) | collective-permute-done | bytes 131104 | tf_op jit(solution)/shard_map/ppermute | solution.py:366
  57.4 0.6 regroup.1
  58.0 4.6 %all-to-all-done.1 = f32[32,1,2176]{2,1,0:T(1,128)S(1)} async-done(((f32[32,1,2176]{2,1,0:T(1,128)}), f32[32,1,2176]{2,1,0:T(1,128)S(1)}, u32[]{:S(2)}, u32[]{:S(2)}) %all-to-all-start.1) | async-done | bytes 278560 | tf_op jit(solution)/shard_map/all_to_all | solution.py:381
  62.6 0.7 scan.1
  63.4 9.6 %all-to-all-start.2 = ((f32[32,16,128]{2,1,0:T(8,128)}), f32[32,16,128]{2,1,0:T(8,128)S(1)}, u32[]{:S(2)}, u32[]{:S(2)}) async-start(f32[32,16,128]{2,1,0:T(8,128)} %scan.1), calls=%async_computation.2 | async-start | bytes 524288 | tf_op jit(solution)/shard_map/all_to_all | solution.py:426
  73.0 3.9 %collective-permute-start.4 = (bf16[4,32,512]{2,1,0:T(8,128)(2,1)S(1)}, bf16[4,32,512]{2,1,0:T(8,128)(2,1)S(1)}, u32[]{:S(2)}, u32[]{:S(2)}) collective-permute-start(bf16[4,32,512]{2,1,0:T(8,128)(2,1)S(1)} %get-tuple-element.44), channel_id=1, source_target_pairs={{0,1},{1,0},{2,3},{3,2},{4,5},{5,4},{6,7},{7,6},{8,9},{9,8},{10,11... | collective-permute-start | bytes 393224 | tf_op jit(solution)/shard_map/ppermute | solution.py:398
  77.0 2.2 %collective-permute-start.5 = (bf16[4,32,512]{2,1,0:T(8,128)(2,1)S(1)}, bf16[4,32,512]{2,1,0:T(8,128)(2,1)S(1)}, u32[]{:S(2)}, u32[]{:S(2)}) collective-permute-start(bf16[4,32,512]{2,1,0:T(8,128)(2,1)S(1)} %get-tuple-element.45), channel_id=1, source_target_pairs={{0,8},{1,9},{2,10},{3,11},{4,12},{5,13},{6,14},{7,15},{8,0},{9,1},... | collective-permute-start | bytes 393224 | tf_op jit(solution)/shard_map/ppermute | solution.py:398
  79.2 3.3 %collective-permute-start.6 = (bf16[4,32,512]{2,1,0:T(8,128)(2,1)S(1)}, bf16[4,32,512]{2,1,0:T(8,128)(2,1)S(1)}, u32[]{:S(2)}, u32[]{:S(2)}) collective-permute-start(bf16[4,32,512]{2,1,0:T(8,128)(2,1)S(1)} %get-tuple-element.46), channel_id=1, source_target_pairs={{0,9},{1,8},{2,11},{3,10},{4,13},{5,12},{6,15},{7,14},{8,1},{9,0},... | collective-permute-start | bytes 393224 | tf_op jit(solution)/shard_map/ppermute | solution.py:398
  82.4 0.0 collective-permute-done.4.refs_1_
  82.4 5.6 %collective-permute-done.5.refs_2_ = bf16[4,32,512]{2,1,0:T(8,128)(2,1)S(1)} collective-permute-done((bf16[4,32,512]{2,1,0:T(8,128)(2,1)S(1)}, bf16[4,32,512]{2,1,0:T(8,128)(2,1)S(1)}, u32[]{:S(2)}, u32[]{:S(2)}) %collective-permute-start.5) | collective-permute-done | bytes 131104 | tf_op jit(solution)/shard_map/ppermute | solution.py:398
  88.0 3.9 %collective-permute-done.6.refs_3_ = bf16[4,32,512]{2,1,0:T(8,128)(2,1)S(1)} collective-permute-done((bf16[4,32,512]{2,1,0:T(8,128)(2,1)S(1)}, bf16[4,32,512]{2,1,0:T(8,128)(2,1)S(1)}, u32[]{:S(2)}, u32[]{:S(2)}) %collective-permute-start.6) | collective-permute-done | bytes 131104 | tf_op jit(solution)/shard_map/ppermute | solution.py:398
  92.0 0.6 settle.1.q_ref
  92.5 2.9 %near.1 = (f32[4,512,128]{2,1,0:T(8,128)S(1)}, bf16[4,512,256]{2,1,0:T(8,128)(2,1)S(1)}) custom-call(bf16[16,32,512]{2,1,0:T(8,128)(2,1)S(1)} %settle.1.q_ref, bf16[16,2,32,512]{3,2,1,0:T(8,128)(2,1)S(1)} %all-to-all-done.part_ref, f32[128,128]{1,0:T(8,128)S(1)} %get-tuple-element.47.rows_ref, f32[128,128]{1,0:T(8,128)S(1)} %get-tuple-element.48.cols_ref), custom_call_target="tpu_custom_call" | custom-call | flops 500000000 | bytes 4000000 | tf_op jit(solution)/shard_map/near/pallas_call | solution.py:417
  95.4 0.0 all-to-all-done.2
  95.5 0.8 close.1
  96.3 14.6 %all_to_all.20.in_ref = bf16[16,32,512]{2,1,0:T(8,128)(2,1)S(1)} all-to-all(bf16[16,32,512]{2,1,0:T(8,128)(2,1)S(1)} %close.1), channel_id=1, replica_groups={{0,1,2,3,4,5,6,7,8,9,10,11,12,13,14,15},{16,17,18,19,20,21,22,23,24,25,..., dimensions={0} | all-to-all | bytes 1048576 | tf_op jit(solution)/shard_map/all_to_all | solution.py:437
  110.9 0.8 unpack.1
Async XLA Ops:
  2.2 10.5 %copy-start.1 = (f32[8,256]{1,0:T(8,128)S(1)}, f32[8,256]{1,0:T(8,128)}, u32[]{:S(2)}) copy-start(f32[8,256]{1,0:T(8,128)} %own_ref.1) | copy-start | bytes 24580
  2.2 13.9 %copy-start = (bf16[32,8192]{1,0:T(8,128)(2,1)S(1)}, bf16[32,8192]{1,0:T(8,128)(2,1)}, u32[]{:S(2)}) copy-start(bf16[32,8192]{1,0:T(8,128)(2,1)} %q_ref.1) | copy-start | bytes 1572868
  2.2 26.4 %all-to-all-start = ((bf16[16,2,32,512]{3,2,1,0:T(8,128)(2,1)}), bf16[16,2,32,512]{3,2,1,0:T(8,128)(2,1)S(1)}, u32[]{:S(2)}, u32[]{:S(2)}) async-start(bf16[16,2,32,512]{3,2,1,0:T(8,128)(2,1)} %pack.1), calls=%async_computation | async-start | bytes 2097152 | tf_op jit(solution)/shard_map/all_to_all | solution.py:334
  12.6 13.6 %collective-permute-start = (f32[8,256]{1,0:T(8,128)S(1)}, f32[8,256]{1,0:T(8,128)S(1)}, u32[]{:S(2)}, u32[]{:S(2)}) collective-permute-start(f32[8,256]{1,0:T(8,128)S(1)} %copy-done.1), channel_id=1, source_target_pairs={{0,8},{8,0},{16,24},{24,16},{32,40},{40,32},{48,56},{56,48},{64,72... | collective-permute-start | bytes 24584 | tf_op jit(solution)/shard_map/ppermute | solution.py:319
  16.1 12.4 %copy-start.2 = (f32[1024]{0:T(1024)S(1)}, f32[1024]{0:T(1024)}, u32[]{:S(2)}) copy-start(f32[1024]{0:T(1024)} %param.11) | copy-start | bytes 12292
  16.9 11.7 %copy-start.3 = (s32[32]{0:T(128)S(1)}, s32[32]{0:T(128)}, u32[]{:S(2)}) copy-start(s32[32]{0:T(128)} %lengths_ref.1) | copy-start | bytes 388
  30.5 32.2 %all-to-all-start.1 = ((f32[32,1,2176]{2,1,0:T(1,128)}), f32[32,1,2176]{2,1,0:T(1,128)S(1)}, u32[]{:S(2)}, u32[]{:S(2)}) async-start(f32[32,1,2176]{2,1,0:T(1,128)} %bitcast.5), calls=%async_computation.1 | async-start | bytes 557056 | tf_op jit(solution)/shard_map/all_to_all | solution.py:381
  44.2 8.8 %collective-permute-start.1 = (bf16[32,2048]{1,0:T(8,128)(2,1)S(1)}, bf16[32,2048]{1,0:T(8,128)(2,1)S(1)}, u32[]{:S(2)}, u32[]{:S(2)}) collective-permute-start(bf16[32,2048]{1,0:T(8,128)(2,1)S(1)} %get-tuple-element.36), channel_id=1, source_target_pairs={{0,2},{1,3},{2,4},{3,5},{4,6},{5,7},{6,0},{7,1},{8,10},{9,11},{10,... | collective-permute-start | bytes 393224 | tf_op jit(solution)/shard_map/ppermute | solution.py:366
  46.1 9.0 %collective-permute-start.2 = (bf16[32,2048]{1,0:T(8,128)(2,1)S(1)}, bf16[32,2048]{1,0:T(8,128)(2,1)S(1)}, u32[]{:S(2)}, u32[]{:S(2)}) collective-permute-start(bf16[32,2048]{1,0:T(8,128)(2,1)S(1)} %get-tuple-element.37), channel_id=1, source_target_pairs={{0,4},{1,5},{2,6},{3,7},{4,0},{5,1},{6,2},{7,3},{8,12},{9,13},{10,... | collective-permute-start | bytes 393224 | tf_op jit(solution)/shard_map/ppermute | solution.py:366
  51.0 6.4 %collective-permute-start.3 = (bf16[32,2048]{1,0:T(8,128)(2,1)S(1)}, bf16[32,2048]{1,0:T(8,128)(2,1)S(1)}, u32[]{:S(2)}, u32[]{:S(2)}) collective-permute-start(bf16[32,2048]{1,0:T(8,128)(2,1)S(1)} %get-tuple-element.38), channel_id=1, source_target_pairs={{0,6},{1,7},{2,0},{3,1},{4,2},{5,3},{6,4},{7,5},{8,14},{9,15},{10,... | collective-permute-start | bytes 393224 | tf_op jit(solution)/shard_map/ppermute | solution.py:366
  63.4 32.1 %all-to-all-start.2 = ((f32[32,16,128]{2,1,0:T(8,128)}), f32[32,16,128]{2,1,0:T(8,128)S(1)}, u32[]{:S(2)}, u32[]{:S(2)}) async-start(f32[32,16,128]{2,1,0:T(8,128)} %scan.1), calls=%async_computation.2 | async-start | bytes 524288 | tf_op jit(solution)/shard_map/all_to_all | solution.py:426
  73.0 9.4 %collective-permute-start.4 = (bf16[4,32,512]{2,1,0:T(8,128)(2,1)S(1)}, bf16[4,32,512]{2,1,0:T(8,128)(2,1)S(1)}, u32[]{:S(2)}, u32[]{:S(2)}) collective-permute-start(bf16[4,32,512]{2,1,0:T(8,128)(2,1)S(1)} %get-tuple-element.44), channel_id=1, source_target_pairs={{0,1},{1,0},{2,3},{3,2},{4,5},{5,4},{6,7},{7,6},{8,9},{9,8},{10,11... | collective-permute-start | bytes 393224 | tf_op jit(solution)/shard_map/ppermute | solution.py:398
  77.0 11.1 %collective-permute-start.5 = (bf16[4,32,512]{2,1,0:T(8,128)(2,1)S(1)}, bf16[4,32,512]{2,1,0:T(8,128)(2,1)S(1)}, u32[]{:S(2)}, u32[]{:S(2)}) collective-permute-start(bf16[4,32,512]{2,1,0:T(8,128)(2,1)S(1)} %get-tuple-element.45), channel_id=1, source_target_pairs={{0,8},{1,9},{2,10},{3,11},{4,12},{5,13},{6,14},{7,15},{8,0},{9,1},... | collective-permute-start | bytes 393224 | tf_op jit(solution)/shard_map/ppermute | solution.py:398
  79.2 12.8 %collective-permute-start.6 = (bf16[4,32,512]{2,1,0:T(8,128)(2,1)S(1)}, bf16[4,32,512]{2,1,0:T(8,128)(2,1)S(1)}, u32[]{:S(2)}, u32[]{:S(2)}) collective-permute-start(bf16[4,32,512]{2,1,0:T(8,128)(2,1)S(1)} %get-tuple-element.46), channel_id=1, source_target_pairs={{0,9},{1,8},{2,11},{3,10},{4,13},{5,12},{6,15},{7,14},{8,1},{9,0},... | collective-permute-start | bytes 393224 | tf_op jit(solution)/shard_map/ppermute | solution.py:398

commit v5 on v4

--- a/solution.py
+++ b/solution.py
@@ -96,12 +96,12 @@
         copy.wait()
 
 
-def slab_kernel(place_ref, q_ref, *refs):
+def slab_kernel(q_ref, *refs):
     outs, sems = refs[:XS], refs[XS]
     width = GROUP // XS * NH * DH
     copies = []
     for turn in range(XS):
-        goal = lax.rem(place_ref[2] + turn, XS)
+        goal = lax.rem(whereabouts()[2] + turn, XS)
         columns = pl.ds(pl.multiple_of(goal * width, width), width)
         copies.append(pltpu.make_async_copy(q_ref.at[:, columns], outs[turn], sems.at[turn]))
     for copy in copies:
@@ -110,8 +110,8 @@
         copy.wait()
 
 
-def regroup_kernel(place_ref, *refs):
-    half, across, core = place_ref[1], place_ref[2], place_ref[3]
+def regroup_kernel(*refs):
+    half, across, core = whereabouts()[1], whereabouts()[2], whereabouts()[3]
     span = NH * DH
     for far, out_ref in enumerate(refs[XS:]):
         goal = 2 * lax.rem(core + far % 2, 2) + lax.rem(half + far // 2, 2)
@@ -121,21 +121,17 @@
             out_ref[origin] = in_ref[:, columns]
 
 
-def settle_kernel(place_ref, *refs):
-    half, core = place_ref[1], place_ref[3]
-    out_ref = refs[-1]
-    for far, in_ref in enumerate(refs[:-1]):
-        start = 8 * lax.rem(half + far // 2, 2) + lax.rem(core + far % 2, 2)
-        for origin in range(XS):
-            out_ref[start + 2 * origin] = in_ref[origin]
+def whereabouts():
+    seq, head = lax.axis_index("seq"), lax.axis_index("head")
+    return seq // PAIR, seq % PAIR, head // 2, head % 2
 
 
 def pick_heads(tile, half):
     return jnp.where(half == 0, tile, pltpu.roll(tile, 4, axis=0))
 
 
-def state_kernel(place_ref, lengths_ref, own_ref, other_ref, part_ref, gain_in_ref, out_ref, rows_ref, cols_ref, gain_ref, send_ref, sems):
-    segment, half = place_ref[0], place_ref[1]
+def state_kernel(lengths_ref, own_ref, other_ref, part_ref, gain_in_ref, out_ref, rows_ref, cols_ref, gain_ref, send_ref, sems):
+    segment, half = whereabouts()[0], whereabouts()[1]
     own, other = own_ref[...], other_ref[...]
     first = jnp.where(half == 0, own, other)
     second = jnp.where(half == 0, other, own)
@@ -181,18 +177,23 @@
     for c in range(NC - 1, 0, -1):
         after.append(after[-1] * carries[c])
     after = after[::-1]
-    rows_ref[0:32] = sums
-    rows_ref[32:64] = jnp.concatenate(tails, axis=0)
-    rows_ref[64:96] = jnp.concatenate(carries, axis=0)
-    rows_ref[96:128] = jnp.concatenate([i.astype(F32) for i in ids[1:]], axis=0)
-    table = jnp.concatenate(
-        [sums]
-        + leads
-        + [lead * b for lead, b in zip(leads, before)]
-        + [i.astype(F32) for i in ids[1:]],
-        axis=0,
-    )
-    cols_ref[...] = table.T
+    floats = [i.astype(F32) for i in ids[1:]]
+    for c in range(NC):
+        for kind, tile in enumerate((sums[8 * c : 8 * c + 8], tails[c], carries[c], floats[c])):
+            rows_ref[c, kind] = tile
+    kinds = (
+        [sums[8 * c : 8 * c + 8] for c in range(NC)],
+        leads,
+        [leads[c] * before[c] for c in range(NC)],
+        floats,
+    )
+    table = [
+        jnp.where(half == 0, tiles[first + i], tiles[2 - first + i])
+        for first in (0, 2)
+        for tiles in kinds
+        for i in range(2)
+    ]
+    cols_ref[...] = jnp.concatenate(table, axis=0).T
 
     full_tails = [t * a for t, a in zip(tails, after)]
     gain_ref[...] = pick_heads(gain_in_ref[...], half)
@@ -216,42 +217,66 @@
         copy.wait()
 
 
-def near_kernel(q_ref, part_ref, rows_ref, cols_ref, near_ref, scaled_ref):
+def chunk_state(part_ref, rows_ref, c, head, keys_across):
+    at = slice(head * DH, (head + 1) * DH)
+    weighted = keys_across.astype(F32) * rows_ref[c, 1, head : head + 1]
+    value_part = part_ref[pl.ds(4 * c, 4), 1, :, at].reshape(CH, DH)
+    both = dot(jnp.concatenate(split2(weighted), axis=0), value_part)
+    return both[:DH] + both[DH:]
+
+
+def keys_of(part_ref, c, head):
+    at = slice(head * DH, (head + 1) * DH)
+    return part_ref[pl.ds(4 * c, 4), 0, :, at].reshape(CH, DH).T
+
+
+def near_half(part, shift, core, same_ref, cross_ref, part_ref, rows_ref, cols_ref, near_ref, scaled_ref):
     order = lax.broadcasted_iota(jnp.int32, (CH, CH), 0) >= lax.broadcasted_iota(
         jnp.int32, (CH, CH), 1
     )
-    cols = cols_ref[...]
-    masks = []
-    for c in range(NC):
-        ids_row = rows_ref[96 + 8 * c : 97 + 8 * c]
-        ids_col = cols[:, 96 + 8 * c : 97 + 8 * c]
-        masks.append(order & (ids_col == ids_row))
+    cols = cols_ref[:, shift : shift + 64]
+    masks = [
+        order & (cols[:, 48 + 8 * i : 49 + 8 * i] == rows_ref[2 * part + i, 3, 0:1])
+        for i in range(2)
+    ]
     for head in range(NH):
         at = slice(head * DH, (head + 1) * DH)
-        state = None
-        for c in range(NC):
-            part = slice(4 * c, 4 * c + 4)
-            row = 8 * c + head
-            query = q_ref[part, :, at].reshape(CH, DH)
-            key_part = part_ref[part, 0, :, at].reshape(CH, DH)
-            value_part = part_ref[part, 1, :, at].reshape(CH, DH)
-            keys_across = key_part.T
-            gaps = cols[:, row : row + 1] - rows_ref[row : row + 1]
-            weights = jnp.where(masks[c], jnp.exp(jnp.where(masks[c], gaps, 0.0)), 0.0)
+        first, second = (
+            chunk_state(part_ref, rows_ref, c, head, keys_of(part_ref, c, head)) for c in range(2)
+        )
+        state = jnp.where(part == 1, second + first * rows_ref[1, 2, head : head + 1], 0.0)
+        for i in range(2):
+            c = 2 * part + i
+            column = 8 * i + head
+            same, cross = (ref[2 * i : 2 * i + 2, :, at] for ref in (same_ref, cross_ref))
+            query = jnp.stack(
+                [jnp.where(core == 0, same, cross), jnp.where(core == 0, cross, same)], axis=1
+            ).reshape(CH, DH)
+            value_part = part_ref[pl.ds(4 * c, 4), 1, :, at].reshape(CH, DH)
+            keys_across = keys_of(part_ref, c, head)
+            gaps = cols[:, column : column + 1] - rows_ref[c, 0, head : head + 1]
+            weights = jnp.where(masks[i], jnp.exp(jnp.where(masks[i], gaps, 0.0)), 0.0)
             high, low = split2(dot(query, keys_across) * weights)
             mixed = dot(high, value_part) + dot(low, value_part)
-            if c:
-                both = dot(query, jnp.concatenate(split2(state), axis=1))
-                mixed = mixed + (both[:, :DH] + both[:, DH:]) * cols[:, 32 + row : 33 + row]
-            near_ref[head, c * CH : (c + 1) * CH] = mixed
-            high, low = split2(query.astype(F32) * cols[:, 64 + row : 65 + row])
-            scaled_ref[head, c * CH : (c + 1) * CH, :DH] = high
-            scaled_ref[head, c * CH : (c + 1) * CH, DH:] = low
-            if c < NC - 1:
-                weighted = keys_across.astype(F32) * rows_ref[32 + row : 33 + row]
-                both = dot(jnp.concatenate(split2(weighted), axis=0), value_part)
-                own = both[:DH] + both[DH:]
-                state = own if c == 0 else own + state * rows_ref[64 + row : 65 + row]
+            both = dot(query, jnp.concatenate(split2(state), axis=1))
+            mixed = mixed + (both[:, :DH] + both[:, DH:]) * cols[:, 16 + column : 17 + column]
+            rows = slice(i * CH, (i + 1) * CH)
+            near_ref[head, rows, :] = mixed
+            high, low = split2(query.astype(F32) * cols[:, 32 + column : 33 + column])
+            scaled_ref[head, rows, :DH] = high
+            scaled_ref[head, rows, DH:] = low
+            if i == 0:
+                state = chunk_state(part_ref, rows_ref, c, head, keys_across) + state * (
+                    rows_ref[c, 2, head : head + 1]
+                )
+
+
+def near_kernel(*refs):
+    near_half(whereabouts()[1], 0, whereabouts()[3], *refs)
+
+
+def rest_kernel(*refs):
+    near_half(1 - whereabouts()[1], 64, whereabouts()[3], *refs)
 
 
 def scan_kernel(in_ref, out_ref, ready, sems):
@@ -273,7 +298,8 @@
         copy.wait()
 
 
-def close_kernel(scaled_ref, state_ref, near_ref, gain_ref, out_ref):
+def close_kernel(state_ref, gain_ref, own_near, own_scaled, other_near, other_scaled, out_ref):
+    half = whereabouts()[1]
     averaging = jnp.full((2 * DH, DH), 1.0 / DH, BF16)
     for head in range(NH):
         high, low = split2(state_ref[head])
@@ -284,13 +310,15 @@
             ],
             axis=0,
         )
-        both = dot(scaled_ref[head], right)
-        mixed = near_ref[head] + (both[:, :DH] + both[:, DH:])
+        both = dot(jnp.concatenate([own_scaled[head], other_scaled[head]], axis=0), right)
+        near = jnp.concatenate([own_near[head], other_near[head]], axis=0)
+        mixed = near + (both[:, :DH] + both[:, DH:])
         square = dot(jnp.concatenate(split2(mixed * mixed), axis=1), averaging)
         normed = mixed * lax.rsqrt(square + 1e-06) * gain_ref[head : head + 1]
-        out_ref[:, :, head * DH : (head + 1) * DH] = normed.astype(BF16).reshape(
-            GROUP, SEG // GROUP, DH
-        )
+        blocks = normed.astype(BF16).reshape(GROUP, SEG // GROUP, DH)
+        at = slice(head * DH, (head + 1) * DH)
+        out_ref[pl.ds(8 * half, 8), :, at] = blocks[:8]
+        out_ref[pl.ds(8 - 8 * half, 8), :, at] = blocks[8:]
 
 
 SMEM = pl.BlockSpec(memory_space=pltpu.SMEM)
@@ -308,9 +336,6 @@
     tokens = queries.shape[0]
     segments = seq_size // PAIR
     pieces = NH * DH // ROWS
-    seq = lax.axis_index("seq")
-    head = lax.axis_index("head")
-    place = jnp.stack([seq // PAIR, seq % PAIR, head // 2, head % 2]).astype(jnp.int32)
     token_groups = [
         [g * GROUP + i for i in range(GROUP)] for g in range(seq_size * head_size // GROUP)
     ]
@@ -338,11 +363,11 @@
         state_kernel,
         out_shape=(
             shaped((pieces * PIECE, DH)),
-            shaped((128, CH)),
+            shaped((NC, 4, 8, CH)),
             shaped((CH, 128)),
             shaped((8, DH)),
         ),
-        in_specs=[SMEM, SMEM, VMEM, VMEM, VMEM, VMEM],
+        in_specs=[SMEM, VMEM, VMEM, VMEM, VMEM],
         out_specs=(ANY, VMEM, VMEM, VMEM),
         scratch_shapes=[
             pltpu.VMEM((pieces * PIECE, DH), F32),
@@ -350,17 +375,17 @@
         ],
         compiler_params=PARAMS,
         name="state",
-    )(place, doc_lengths, log_decay, other_decay, parts, gain.reshape(8, DH))
+    )(doc_lengths, log_decay, other_decay, parts, gain.reshape(8, DH))
     span = GROUP // XS * NH * DH
     slabs = pl.pallas_call(
         slab_kernel,
         out_shape=[shaped((tokens, span), BF16)] * XS,
-        in_specs=[SMEM, ANY],
+        in_specs=[ANY],
         out_specs=[VMEM] * XS,
         scratch_shapes=[pltpu.SemaphoreType.DMA((XS,))],
         compiler_params=PARAMS,
         name="slab",
-    )(place, queries)
+    )(queries)
     slabs, own = lax.optimization_barrier((slabs, own))
     turned = [slabs[0]] + [
         lax.ppermute(
@@ -373,11 +398,11 @@
     grouped = pl.pallas_call(
         regroup_kernel,
         out_shape=[shaped((XS, tokens, NH * DH), BF16)] * 4,
-        in_specs=[SMEM] + [VMEM] * XS,
+        in_specs=[VMEM] * XS,
         out_specs=[VMEM] * 4,
         compiler_params=PARAMS,
         name="regroup",
-    )(place, *turned)
+    )(*turned)
     gathered = lax.all_to_all(
         own.reshape(pieces, 1, PIECE * DH), "seq", 0, 0, axis_index_groups=scan_groups, tiled=True
     ).reshape(pieces * PIECE, DH)
@@ -406,34 +431,33 @@
         )
         for far in range(1, 4)
     ]
-    query_parts = pl.pallas_call(
-        settle_kernel,
-        out_shape=shaped((GROUP, tokens, NH * DH), BF16),
-        in_specs=[SMEM] + [VMEM] * 4,
-        out_specs=VMEM,
-        compiler_params=PARAMS,
-        name="settle",
-    )(place, *swapped)
-    near, scaled = pl.pallas_call(
-        near_kernel,
-        out_shape=(shaped((NH, SEG, DH)), shaped((NH, SEG, 2 * DH), BF16)),
-        in_specs=[VMEM, VMEM, VMEM, VMEM],
-        out_specs=(VMEM, VMEM),
-        compiler_params=PARAMS,
-        cost_estimate=pl.CostEstimate(flops=500000000, transcendentals=300000, bytes_accessed=4000000),
-        name="near",
-    )(query_parts, parts, rows, cols)
+
+    def near_call(kernel, name, same, cross):
+        return pl.pallas_call(
+            kernel,
+            out_shape=(shaped((NH, SEG // 2, DH)), shaped((NH, SEG // 2, 2 * DH), BF16)),
+            in_specs=[VMEM] * 5,
+            out_specs=(VMEM, VMEM),
+            compiler_params=PARAMS,
+            cost_estimate=pl.CostEstimate(
+                flops=250000000, transcendentals=150000, bytes_accessed=3000000
+            ),
+            name=name,
+        )(same, cross, parts, rows, cols)
+
+    near = near_call(near_kernel, "near", swapped[0], swapped[1])
+    rest = near_call(rest_kernel, "rest", swapped[2], swapped[3])
     incoming = lax.all_to_all(
         prefixes, "seq", 0, 0, axis_index_groups=scan_groups, tiled=True
     ).reshape(NH, DH, DH)
     normed = pl.pallas_call(
         close_kernel,
         out_shape=shaped((GROUP, tokens, NH * DH), BF16),
-        in_specs=[VMEM] * 4,
+        in_specs=[VMEM] * 6,
         out_specs=VMEM,
         compiler_params=PARAMS,
         name="close",
-    )(scaled, incoming, near, gains)
+    )(incoming, gains, *near, *rest)
     returned = lax.all_to_all(
         normed, ("seq", "head"), 0, 0, axis_index_groups=token_groups, tiled=True
     )

time: 112 us -> 111 us (level)
    ppermute x3, waiting for transfers between devices: 9.51 us -> 7.91 us  [local(): lax.ppermute(grouped[far], ('seq', 'head'), [(s * head_size + h, (s ^ far...]
  transfers between devices with their start and end apart: 10 -> 10, of which waited for: 7 -> 7; matrix products, arithmetic and copies ran while one was open for 0% -> 0% of each run, Pallas kernels for 4% -> 3%
where the time goes in v5:
time: 111 us
  starting transfers between devices  54.7 us (49%)
  waiting for transfers between devices  29.8 us (27%)
  blocking collectives  15.5 us (14%)
  Pallas kernels  10.3 us (9%)
    all_to_all x1, blocking collectives, local(): lax.all_to_all(normed, ('seq', 'head'), 0, 0, axis_index_groups=token_gro...  15.5 us
    all_to_all x1, starting transfers between devices, local(): lax.all_to_all(own.reshape(pieces, 1, PIECE * DH), 'seq', 0, 0, axis_inde...  13.7 us
    all_to_all x1, starting transfers between devices, local(): lax.all_to_all(sent, ('seq', 'head'), 0, 0, axis_index_groups=token_group...  10.5 us
    ppermute x1, waiting for transfers between devices, local(): lax.ppermute(log_decay, 'seq', [(s, s ^ 1) for s in range(seq_size)])  9.97 us
    all_to_all x1, starting transfers between devices, local(): lax.all_to_all(prefixes, 'seq', 0, 0, axis_index_groups=scan_groups, tile...  9.4 us
    ppermute x3, starting transfers between devices, local(): lax.ppermute(grouped[far], ('seq', 'head'), [(s * head_size + h, (s ^ far...  9.07 us
    ppermute x3, starting transfers between devices, local(): lax.ppermute(slabs[turn], 'head', [(h, (h // 2 + turn) % XS * 2 + h % 2)...  8.75 us
    ppermute x3, waiting for transfers between devices, local(): lax.ppermute(grouped[far], ('seq', 'head'), [(s * head_size + h, (s ^ far...  7.91 us
  transfers between devices with their start and end apart: 10, of which 7 were waited for; matrix products, arithmetic and copies ran while one was open for 0% of the time, Pallas kernels for 3%

profile of v5, /device:TPU:1, one launch (start us, length us, event | category | flops | bytes accessed | tf_op | source)
XLA Modules:
  0.0 110.6 jit_solution(7602985864439844220)
XLA Ops:
  0.0 2.1 %pack.1 = bf16[16,2,32,512]{3,2,1,0:T(8,128)(2,1)} custom-call(bf16[32,8192]{1,0:T(8,128)(2,1)} %k_ref.1, bf16[32,8192]{1,0:T(8,128)(2,1)} %v_ref.1), custom_call_target="tpu_custom_call" | custom-call | tf_op jit(solution)/shard_map/pack/pallas_call | solution.py:345
  2.2 0.0 copy-start.1
  2.2 0.0 copy-start
  2.2 10.5 %all-to-all-start = ((bf16[16,2,32,512]{3,2,1,0:T(8,128)(2,1)}), bf16[16,2,32,512]{3,2,1,0:T(8,128)(2,1)S(1)}, u32[]{:S(2)}, u32[]{:S(2)}) async-start(bf16[16,2,32,512]{3,2,1,0:T(8,128)(2,1)} %pack.1), calls=%async_computation | async-start | bytes 2097152 | tf_op jit(solution)/shard_map/all_to_all | solution.py:359
  12.6 0.0 copy-done.1
  12.6 3.3 %collective-permute-start = (f32[8,256]{1,0:T(8,128)S(1)}, f32[8,256]{1,0:T(8,128)S(1)}, u32[]{:S(2)}, u32[]{:S(2)}) collective-permute-start(f32[8,256]{1,0:T(8,128)S(1)} %copy-done.1), channel_id=1, source_target_pairs={{0,8},{8,0},{16,24},{24,16},{32,40},{40,32},{48,56},{56,48},{64,72... | collective-permute-start | bytes 24584 | tf_op jit(solution)/shard_map/ppermute | solution.py:344
  16.0 0.0 copy-done
  16.0 0.0 copy-start.2
  16.0 0.2 slab.1
  16.3 0.0 copy-start.3
  16.3 10.0 %collective-permute-done.other_ref = f32[8,256]{1,0:T(8,128)S(1)} collective-permute-done((f32[8,256]{1,0:T(8,128)S(1)}, f32[8,256]{1,0:T(8,128)S(1)}, u32[]{:S(2)}, u32[]{:S(2)}) %collective-permute-start) | collective-permute-done | bytes 8224 | tf_op jit(solution)/shard_map/ppermute | solution.py:344
  26.2 2.3 %all-to-all-done.part_ref.refs_2_ = bf16[16,2,32,512]{3,2,1,0:T(8,128)(2,1)S(1)} async-done(((bf16[16,2,32,512]{3,2,1,0:T(8,128)(2,1)}), bf16[16,2,32,512]{3,2,1,0:T(8,128)(2,1)S(1)}, u32[]{:S(2)}, u32[]{:S(2)}) %all-to-all-start) | async-done | bytes 1048608 | tf_op jit(solution)/shard_map/all_to_all | solution.py:359
  28.5 0.0 copy-done.2
  28.6 0.0 copy-done.3
  28.6 1.9 %state.1 = (f32[544,128]{1,0:T(8,128)}, f32[4,4,8,128]{3,2,1,0:T(8,128)S(1)}, f32[128,128]{1,0:T(8,128)S(1)}, f32[8,128]{1,0:T(8,128)S(1)}) custom-call(s32[32]{0:T(128)S(1)} %copy-done.3, f32[8,256]{1,0:T(8,128)S(1)} %copy-done.1, f32[8,256]{1,0:T(8,128)S(1)} %collective-permute-done.other_ref, bf16[16,2,32,512]{3,2,1,0:T(8,128)(2,1)S(1)} %all-to-all-done.part_ref.refs_2_, ...), custom_call_target="tpu_custom_call" | custom-call | tf_op jit(solution)/shard_map/state/pallas_call | solution.py:362
  30.5 13.7 %all-to-all-start.1 = ((f32[32,1,2176]{2,1,0:T(1,128)}), f32[32,1,2176]{2,1,0:T(1,128)S(1)}, u32[]{:S(2)}, u32[]{:S(2)}) async-start(f32[32,1,2176]{2,1,0:T(1,128)} %bitcast.1), calls=%async_computation.1 | async-start | bytes 557056 | tf_op jit(solution)/shard_map/all_to_all | solution.py:406
  44.2 1.9 %collective-permute-start.1 = (bf16[32,2048]{1,0:T(8,128)(2,1)S(1)}, bf16[32,2048]{1,0:T(8,128)(2,1)S(1)}, u32[]{:S(2)}, u32[]{:S(2)}) collective-permute-start(bf16[32,2048]{1,0:T(8,128)(2,1)S(1)} %get-tuple-element.38), channel_id=1, source_target_pairs={{0,2},{1,3},{2,4},{3,5},{4,6},{5,7},{6,0},{7,1},{8,10},{9,11},{10,... | collective-permute-start | bytes 393224 | tf_op jit(solution)/shard_map/ppermute | solution.py:391
  46.1 4.9 %collective-permute-start.2 = (bf16[32,2048]{1,0:T(8,128)(2,1)S(1)}, bf16[32,2048]{1,0:T(8,128)(2,1)S(1)}, u32[]{:S(2)}, u32[]{:S(2)}) collective-permute-start(bf16[32,2048]{1,0:T(8,128)(2,1)S(1)} %get-tuple-element.39), channel_id=1, source_target_pairs={{0,4},{1,5},{2,6},{3,7},{4,0},{5,1},{6,2},{7,3},{8,12},{9,13},{10,... | collective-permute-start | bytes 393224 | tf_op jit(solution)/shard_map/ppermute | solution.py:391
  51.0 1.9 %collective-permute-start.3 = (bf16[32,2048]{1,0:T(8,128)(2,1)S(1)}, bf16[32,2048]{1,0:T(8,128)(2,1)S(1)}, u32[]{:S(2)}, u32[]{:S(2)}) collective-permute-start(bf16[32,2048]{1,0:T(8,128)(2,1)S(1)} %get-tuple-element.40), channel_id=1, source_target_pairs={{0,6},{1,7},{2,0},{3,1},{4,2},{5,3},{6,4},{7,5},{8,14},{9,15},{10,... | collective-permute-start | bytes 393224 | tf_op jit(solution)/shard_map/ppermute | solution.py:391
  53.0 0.0 collective-permute-done.1.refs_1_
  53.0 2.1 %collective-permute-done.2.refs_2_ = bf16[32,2048]{1,0:T(8,128)(2,1)S(1)} collective-permute-done((bf16[32,2048]{1,0:T(8,128)(2,1)S(1)}, bf16[32,2048]{1,0:T(8,128)(2,1)S(1)}, u32[]{:S(2)}, u32[]{:S(2)}) %collective-permute-start.2) | collective-permute-done | bytes 131104 | tf_op jit(solution)/shard_map/ppermute | solution.py:391
  55.1 2.4 %collective-permute-done.3.refs_3_ = bf16[32,2048]{1,0:T(8,128)(2,1)S(1)} collective-permute-done((bf16[32,2048]{1,0:T(8,128)(2,1)S(1)}, bf16[32,2048]{1,0:T(8,128)(2,1)S(1)}, u32[]{:S(2)}, u32[]{:S(2)}) %collective-permute-start.3) | collective-permute-done | bytes 131104 | tf_op jit(solution)/shard_map/ppermute | solution.py:391
  57.5 5.2 %all-to-all-done.1 = f32[32,1,2176]{2,1,0:T(1,128)S(1)} async-done(((f32[32,1,2176]{2,1,0:T(1,128)}), f32[32,1,2176]{2,1,0:T(1,128)S(1)}, u32[]{:S(2)}, u32[]{:S(2)}) %all-to-all-start.1) | async-done | bytes 278560 | tf_op jit(solution)/shard_map/all_to_all | solution.py:406
  62.6 0.7 scan.1
  63.4 9.4 %all-to-all-start.2 = ((f32[32,16,128]{2,1,0:T(8,128)}), f32[32,16,128]{2,1,0:T(8,128)S(1)}, u32[]{:S(2)}, u32[]{:S(2)}) async-start(f32[32,16,128]{2,1,0:T(8,128)} %scan.1), calls=%async_computation.2 | async-start | bytes 524288 | tf_op jit(solution)/shard_map/all_to_all | solution.py:450
  72.8 3.6 %collective-permute-start.4 = (bf16[4,32,512]{2,1,0:T(8,128)(2,1)S(1)}, bf16[4,32,512]{2,1,0:T(8,128)(2,1)S(1)}, u32[]{:S(2)}, u32[]{:S(2)}) collective-permute-start(bf16[4,32,512]{2,1,0:T(8,128)(2,1)S(1)} %get-tuple-element.48), channel_id=1, source_target_pairs={{0,1},{1,0},{2,3},{3,2},{4,5},{5,4},{6,7},{7,6},{8,9},{9,8},{10,11... | collective-permute-start | bytes 393224 | tf_op jit(solution)/shard_map/ppermute | solution.py:423
  76.4 2.2 %collective-permute-start.5 = (bf16[4,32,512]{2,1,0:T(8,128)(2,1)S(1)}, bf16[4,32,512]{2,1,0:T(8,128)(2,1)S(1)}, u32[]{:S(2)}, u32[]{:S(2)}) collective-permute-start(bf16[4,32,512]{2,1,0:T(8,128)(2,1)S(1)} %get-tuple-element.53), channel_id=1, source_target_pairs={{0,8},{1,9},{2,10},{3,11},{4,12},{5,13},{6,14},{7,15},{8,0},{9,1},... | collective-permute-start | bytes 393224 | tf_op jit(solution)/shard_map/ppermute | solution.py:423
  78.6 3.3 %collective-permute-start.6 = (bf16[4,32,512]{2,1,0:T(8,128)(2,1)S(1)}, bf16[4,32,512]{2,1,0:T(8,128)(2,1)S(1)}, u32[]{:S(2)}, u32[]{:S(2)}) collective-permute-start(bf16[4,32,512]{2,1,0:T(8,128)(2,1)S(1)} %get-tuple-element.54), channel_id=1, source_target_pairs={{0,9},{1,8},{2,11},{3,10},{4,13},{5,12},{6,15},{7,14},{8,1},{9,0},... | collective-permute-start | bytes 393224 | tf_op jit(solution)/shard_map/ppermute | solution.py:423
  81.9 0.0 collective-permute-done.4.refs_1_
  81.9 1.8 %near.1 = (f32[4,256,128]{2,1,0:T(8,128)S(1)}, bf16[4,256,256]{2,1,0:T(8,128)(2,1)S(1)}) custom-call(bf16[4,32,512]{2,1,0:T(8,128)(2,1)S(1)} %get-tuple-element.47.refs_0_, bf16[4,32,512]{2,1,0:T(8,128)(2,1)S(1)} %collective-permute-done.4.refs_1_, bf16[16,2,32,512]{3,2,1,0:T(8,128)(2,1)S(1)} %all-to-all-done.part_ref.refs_2_, ...), custom_call_target="tpu_custom_call" | custom-call | flops 250000000 | bytes 3000000 | tf_op jit(solution)/shard_map/near/pallas_call | solution.py:436
  83.7 4.1 %collective-permute-done.5.refs_0_ = bf16[4,32,512]{2,1,0:T(8,128)(2,1)S(1)} collective-permute-done((bf16[4,32,512]{2,1,0:T(8,128)(2,1)S(1)}, bf16[4,32,512]{2,1,0:T(8,128)(2,1)S(1)}, u32[]{:S(2)}, u32[]{:S(2)}) %collective-permute-start.5) | collective-permute-done | bytes 131104 | tf_op jit(solution)/shard_map/ppermute | solution.py:423
  87.8 3.8 %collective-permute-done.6.refs_1_ = bf16[4,32,512]{2,1,0:T(8,128)(2,1)S(1)} collective-permute-done((bf16[4,32,512]{2,1,0:T(8,128)(2,1)S(1)}, bf16[4,32,512]{2,1,0:T(8,128)(2,1)S(1)}, u32[]{:S(2)}, u32[]{:S(2)}) %collective-permute-start.6) | collective-permute-done | bytes 131104 | tf_op jit(solution)/shard_map/ppermute | solution.py:423
  91.6 1.8 %rest.1 = (f32[4,256,128]{2,1,0:T(8,128)S(1)}, bf16[4,256,256]{2,1,0:T(8,128)(2,1)S(1)}) custom-call(bf16[4,32,512]{2,1,0:T(8,128)(2,1)S(1)} %collective-permute-done.5.refs_0_, bf16[4,32,512]{2,1,0:T(8,128)(2,1)S(1)} %collective-permute-done.6.refs_1_, bf16[16,2,32,512]{3,2,1,0:T(8,128)(2,1)S(1)} %all-to-all-done.part_ref.refs_2_, ...), custom_call_target="tpu_custom_call" | custom-call | flops 250000000 | bytes 3000000 | tf_op jit(solution)/shard_map/rest/pallas_call | solution.py:436
  93.4 0.0 all-to-all-done.2
  93.4 0.8 close.1
  94.3 15.5 %all_to_all.20.in_ref = bf16[16,32,512]{2,1,0:T(8,128)(2,1)S(1)} all-to-all(bf16[16,32,512]{2,1,0:T(8,128)(2,1)S(1)} %close.1), channel_id=1, replica_groups={{0,1,2,3,4,5,6,7,8,9,10,11,12,13,14,15},{16,17,18,19,20,21,22,23,24,25,..., dimensions={0} | all-to-all | bytes 1048576 | tf_op jit(solution)/shard_map/all_to_all | solution.py:461
  109.8 0.8 unpack.1
  (1 shorter events, 0.0 us)
Async XLA Ops:
  2.2 10.5 %copy-start.1 = (f32[8,256]{1,0:T(8,128)S(1)}, f32[8,256]{1,0:T(8,128)}, u32[]{:S(2)}) copy-start(f32[8,256]{1,0:T(8,128)} %own_ref.1) | copy-start | bytes 24580
  2.2 13.8 %copy-start = (bf16[32,8192]{1,0:T(8,128)(2,1)S(1)}, bf16[32,8192]{1,0:T(8,128)(2,1)}, u32[]{:S(2)}) copy-start(bf16[32,8192]{1,0:T(8,128)(2,1)} %q_ref.1) | copy-start | bytes 1572868
  2.2 26.4 %all-to-all-start = ((bf16[16,2,32,512]{3,2,1,0:T(8,128)(2,1)}), bf16[16,2,32,512]{3,2,1,0:T(8,128)(2,1)S(1)}, u32[]{:S(2)}, u32[]{:S(2)}) async-start(bf16[16,2,32,512]{3,2,1,0:T(8,128)(2,1)} %pack.1), calls=%async_computation | async-start | bytes 2097152 | tf_op jit(solution)/shard_map/all_to_all | solution.py:359
  12.6 13.6 %collective-permute-start = (f32[8,256]{1,0:T(8,128)S(1)}, f32[8,256]{1,0:T(8,128)S(1)}, u32[]{:S(2)}, u32[]{:S(2)}) collective-permute-start(f32[8,256]{1,0:T(8,128)S(1)} %copy-done.1), channel_id=1, source_target_pairs={{0,8},{8,0},{16,24},{24,16},{32,40},{40,32},{48,56},{56,48},{64,72... | collective-permute-start | bytes 24584 | tf_op jit(solution)/shard_map/ppermute | solution.py:344
  16.0 12.5 %copy-start.2 = (f32[1024]{0:T(1024)S(1)}, f32[1024]{0:T(1024)}, u32[]{:S(2)}) copy-start(f32[1024]{0:T(1024)} %param.11) | copy-start | bytes 12292
  16.3 12.3 %copy-start.3 = (s32[32]{0:T(128)S(1)}, s32[32]{0:T(128)}, u32[]{:S(2)}) copy-start(s32[32]{0:T(128)} %lengths_ref.1) | copy-start | bytes 388
  30.5 32.2 %all-to-all-start.1 = ((f32[32,1,2176]{2,1,0:T(1,128)}), f32[32,1,2176]{2,1,0:T(1,128)S(1)}, u32[]{:S(2)}, u32[]{:S(2)}) async-start(f32[32,1,2176]{2,1,0:T(1,128)} %bitcast.1), calls=%async_computation.1 | async-start | bytes 557056 | tf_op jit(solution)/shard_map/all_to_all | solution.py:406
  44.2 8.8 %collective-permute-start.1 = (bf16[32,2048]{1,0:T(8,128)(2,1)S(1)}, bf16[32,2048]{1,0:T(8,128)(2,1)S(1)}, u32[]{:S(2)}, u32[]{:S(2)}) collective-permute-start(bf16[32,2048]{1,0:T(8,128)(2,1)S(1)} %get-tuple-element.38), channel_id=1, source_target_pairs={{0,2},{1,3},{2,4},{3,5},{4,6},{5,7},{6,0},{7,1},{8,10},{9,11},{10,... | collective-permute-start | bytes 393224 | tf_op jit(solution)/shard_map/ppermute | solution.py:391
  46.1 9.0 %collective-permute-start.2 = (bf16[32,2048]{1,0:T(8,128)(2,1)S(1)}, bf16[32,2048]{1,0:T(8,128)(2,1)S(1)}, u32[]{:S(2)}, u32[]{:S(2)}) collective-permute-start(bf16[32,2048]{1,0:T(8,128)(2,1)S(1)} %get-tuple-element.39), channel_id=1, source_target_pairs={{0,4},{1,5},{2,6},{3,7},{4,0},{5,1},{6,2},{7,3},{8,12},{9,13},{10,... | collective-permute-start | bytes 393224 | tf_op jit(solution)/shard_map/ppermute | solution.py:391
  51.0 6.4 %collective-permute-start.3 = (bf16[32,2048]{1,0:T(8,128)(2,1)S(1)}, bf16[32,2048]{1,0:T(8,128)(2,1)S(1)}, u32[]{:S(2)}, u32[]{:S(2)}) collective-permute-start(bf16[32,2048]{1,0:T(8,128)(2,1)S(1)} %get-tuple-element.40), channel_id=1, source_target_pairs={{0,6},{1,7},{2,0},{3,1},{4,2},{5,3},{6,4},{7,5},{8,14},{9,15},{10,... | collective-permute-start | bytes 393224 | tf_op jit(solution)/shard_map/ppermute | solution.py:391
  63.4 30.0 %all-to-all-start.2 = ((f32[32,16,128]{2,1,0:T(8,128)}), f32[32,16,128]{2,1,0:T(8,128)S(1)}, u32[]{:S(2)}, u32[]{:S(2)}) async-start(f32[32,16,128]{2,1,0:T(8,128)} %scan.1), calls=%async_computation.2 | async-start | bytes 524288 | tf_op jit(solution)/shard_map/all_to_all | solution.py:450
  72.8 9.1 %collective-permute-start.4 = (bf16[4,32,512]{2,1,0:T(8,128)(2,1)S(1)}, bf16[4,32,512]{2,1,0:T(8,128)(2,1)S(1)}, u32[]{:S(2)}, u32[]{:S(2)}) collective-permute-start(bf16[4,32,512]{2,1,0:T(8,128)(2,1)S(1)} %get-tuple-element.48), channel_id=1, source_target_pairs={{0,1},{1,0},{2,3},{3,2},{4,5},{5,4},{6,7},{7,6},{8,9},{9,8},{10,11... | collective-permute-start | bytes 393224 | tf_op jit(solution)/shard_map/ppermute | solution.py:423
  76.4 11.4 %collective-permute-start.5 = (bf16[4,32,512]{2,1,0:T(8,128)(2,1)S(1)}, bf16[4,32,512]{2,1,0:T(8,128)(2,1)S(1)}, u32[]{:S(2)}, u32[]{:S(2)}) collective-permute-start(bf16[4,32,512]{2,1,0:T(8,128)(2,1)S(1)} %get-tuple-element.53), channel_id=1, source_target_pairs={{0,8},{1,9},{2,10},{3,11},{4,12},{5,13},{6,14},{7,15},{8,0},{9,1},... | collective-permute-start | bytes 393224 | tf_op jit(solution)/shard_map/ppermute | solution.py:423
  78.6 13.0 %collective-permute-start.6 = (bf16[4,32,512]{2,1,0:T(8,128)(2,1)S(1)}, bf16[4,32,512]{2,1,0:T(8,128)(2,1)S(1)}, u32[]{:S(2)}, u32[]{:S(2)}) collective-permute-start(bf16[4,32,512]{2,1,0:T(8,128)(2,1)S(1)} %get-tuple-element.54), channel_id=1, source_target_pairs={{0,9},{1,8},{2,11},{3,10},{4,13},{5,12},{6,15},{7,14},{8,1},{9,0},... | collective-permute-start | bytes 393224 | tf_op jit(solution)/shard_map/ppermute | solution.py:423

commit v6 on v5

--- a/solution.py
+++ b/solution.py
@@ -153,9 +153,12 @@
     start = segment * SEG
     spots = [jnp.full((8, CH), start - 1, jnp.int32)] + [start + c * CH + lane for c in range(NC)]
     ids = [jnp.zeros((8, CH), jnp.int32) for _ in spots]
-    end = jnp.int32(0)
-    for d in range(lengths_ref.shape[0]):
-        end = end + lengths_ref[d]
+    docs = lengths_ref.shape[1]
+    parts = split3(jnp.broadcast_to(lengths_ref[...].astype(F32), (8, docs)))
+    high, mid, low = (dot(part, upper[:docs, :docs]) for part in parts)
+    ends = (high + (mid + low)).astype(jnp.int32)
+    for d in range(docs):
+        end = jnp.broadcast_to(ends[:, d : d + 1], (8, CH))
         ids = [i + (end <= s).astype(jnp.int32) for i, s in zip(ids, spots)]
 
     def last(tile):
@@ -367,7 +370,7 @@
             shaped((CH, 128)),
             shaped((8, DH)),
         ),
-        in_specs=[SMEM, VMEM, VMEM, VMEM, VMEM],
+        in_specs=[VMEM, VMEM, VMEM, VMEM, VMEM],
         out_specs=(ANY, VMEM, VMEM, VMEM),
         scratch_shapes=[
             pltpu.VMEM((pieces * PIECE, DH), F32),
@@ -375,7 +378,7 @@
         ],
         compiler_params=PARAMS,
         name="state",
-    )(doc_lengths, log_decay, other_decay, parts, gain.reshape(8, DH))
+    )(doc_lengths.reshape(1, -1), log_decay, other_decay, parts, gain.reshape(8, DH))
     span = GROUP // XS * NH * DH
     slabs = pl.pallas_call(
         slab_kernel,

time: 111 us -> 111 us (level)
  no operation moved by 1% of the time
where the time goes in v6:
time: 111 us
  starting transfers between devices  54.7 us (49%)
  waiting for transfers between devices  29.8 us (27%)
  blocking collectives  15.5 us (14%)
  Pallas kernels  9.85 us (9%)
    all_to_all x1, blocking collectives, local(): lax.all_to_all(normed, ('seq', 'head'), 0, 0, axis_index_groups=token_gro...  15.5 us
    all_to_all x1, starting transfers between devices, local(): lax.all_to_all(own.reshape(pieces, 1, PIECE * DH), 'seq', 0, 0, axis_inde...  13.7 us
    all_to_all x1, starting transfers between devices, local(): lax.all_to_all(sent, ('seq', 'head'), 0, 0, axis_index_groups=token_group...  10.5 us
    ppermute x1, waiting for transfers between devices, local(): lax.ppermute(log_decay, 'seq', [(s, s ^ 1) for s in range(seq_size)])  9.99 us
    all_to_all x1, starting transfers between devices, local(): lax.all_to_all(prefixes, 'seq', 0, 0, axis_index_groups=scan_groups, tile...  9.4 us
    ppermute x3, starting transfers between devices, local(): lax.ppermute(grouped[far], ('seq', 'head'), [(s * head_size + h, (s ^ far...  9.07 us
    ppermute x3, starting transfers between devices, local(): lax.ppermute(slabs[turn], 'head', [(h, (h // 2 + turn) % XS * 2 + h % 2)...  8.75 us
    ppermute x3, waiting for transfers between devices, local(): lax.ppermute(grouped[far], ('seq', 'head'), [(s * head_size + h, (s ^ far...  7.91 us
  transfers between devices with their start and end apart: 10, of which 7 were waited for; matrix products, arithmetic and copies ran while one was open for 0% of the time, Pallas kernels for 3%

profile of v6, /device:TPU:1, one launch (start us, length us, event | category | flops | bytes accessed | tf_op | source)
XLA Modules:
  0.0 110.8 jit_solution(15693295216500158672)
XLA Ops:
  0.0 2.1 %pack.1 = bf16[16,2,32,512]{3,2,1,0:T(8,128)(2,1)} custom-call(bf16[32,8192]{1,0:T(8,128)(2,1)} %k_ref.1, bf16[32,8192]{1,0:T(8,128)(2,1)} %v_ref.1), custom_call_target="tpu_custom_call" | custom-call | tf_op jit(solution)/shard_map/pack/pallas_call | solution.py:348
  2.2 0.0 copy-start.1
  2.2 0.0 copy-start
  2.2 10.5 %all-to-all-start = ((bf16[16,2,32,512]{3,2,1,0:T(8,128)(2,1)}), bf16[16,2,32,512]{3,2,1,0:T(8,128)(2,1)S(1)}, u32[]{:S(2)}, u32[]{:S(2)}) async-start(bf16[16,2,32,512]{3,2,1,0:T(8,128)(2,1)} %pack.1), calls=%async_computation | async-start | bytes 2097152 | tf_op jit(solution)/shard_map/all_to_all | solution.py:362
  12.6 0.0 copy-done.1
  12.6 3.3 %collective-permute-start = (f32[8,256]{1,0:T(8,128)S(1)}, f32[8,256]{1,0:T(8,128)S(1)}, u32[]{:S(2)}, u32[]{:S(2)}) collective-permute-start(f32[8,256]{1,0:T(8,128)S(1)} %copy-done.1), channel_id=1, source_target_pairs={{0,8},{8,0},{16,24},{24,16},{32,40},{40,32},{48,56},{56,48},{64,72... | collective-permute-start | bytes 24584 | tf_op jit(solution)/shard_map/ppermute | solution.py:347
  16.0 0.0 copy-done
  16.0 0.0 copy-start.2
  16.0 0.2 slab.1
  16.3 10.0 %collective-permute-done.other_ref = f32[8,256]{1,0:T(8,128)S(1)} collective-permute-done((f32[8,256]{1,0:T(8,128)S(1)}, f32[8,256]{1,0:T(8,128)S(1)}, u32[]{:S(2)}, u32[]{:S(2)}) %collective-permute-start) | collective-permute-done | bytes 8224 | tf_op jit(solution)/shard_map/ppermute | solution.py:347
  26.2 2.3 %all-to-all-done.part_ref.refs_2_ = bf16[16,2,32,512]{3,2,1,0:T(8,128)(2,1)S(1)} async-done(((bf16[16,2,32,512]{3,2,1,0:T(8,128)(2,1)}), bf16[16,2,32,512]{3,2,1,0:T(8,128)(2,1)S(1)}, u32[]{:S(2)}, u32[]{:S(2)}) %all-to-all-start) | async-done | bytes 1048608 | tf_op jit(solution)/shard_map/all_to_all | solution.py:362
  28.5 0.0 copy-start.3
  28.6 0.0 copy-done.2
  28.6 0.7 copy-done.3
  29.2 1.4 %state.1 = (f32[544,128]{1,0:T(8,128)}, f32[4,4,8,128]{3,2,1,0:T(8,128)S(1)}, f32[128,128]{1,0:T(8,128)S(1)}, f32[8,128]{1,0:T(8,128)S(1)}) custom-call(s32[1,32]{1,0:T(1,128)S(1)} %bitcast.8, f32[8,256]{1,0:T(8,128)S(1)} %copy-done.1, f32[8,256]{1,0:T(8,128)S(1)} %collective-permute-done.other_ref, ...), custom_call_target="tpu_custom_call" | custom-call | tf_op jit(solution)/shard_map/state/pallas_call | solution.py:365
  30.7 13.7 %all-to-all-start.1 = ((f32[32,1,2176]{2,1,0:T(1,128)}), f32[32,1,2176]{2,1,0:T(1,128)S(1)}, u32[]{:S(2)}, u32[]{:S(2)}) async-start(f32[32,1,2176]{2,1,0:T(1,128)} %bitcast.2), calls=%async_computation.1 | async-start | bytes 557056 | tf_op jit(solution)/shard_map/all_to_all | solution.py:409
  44.4 1.9 %collective-permute-start.1 = (bf16[32,2048]{1,0:T(8,128)(2,1)S(1)}, bf16[32,2048]{1,0:T(8,128)(2,1)S(1)}, u32[]{:S(2)}, u32[]{:S(2)}) collective-permute-start(bf16[32,2048]{1,0:T(8,128)(2,1)S(1)} %get-tuple-element.38), channel_id=1, source_target_pairs={{0,2},{1,3},{2,4},{3,5},{4,6},{5,7},{6,0},{7,1},{8,10},{9,11},{10,... | collective-permute-start | bytes 393224 | tf_op jit(solution)/shard_map/ppermute | solution.py:394
  46.3 4.9 %collective-permute-start.2 = (bf16[32,2048]{1,0:T(8,128)(2,1)S(1)}, bf16[32,2048]{1,0:T(8,128)(2,1)S(1)}, u32[]{:S(2)}, u32[]{:S(2)}) collective-permute-start(bf16[32,2048]{1,0:T(8,128)(2,1)S(1)} %get-tuple-element.39), channel_id=1, source_target_pairs={{0,4},{1,5},{2,6},{3,7},{4,0},{5,1},{6,2},{7,3},{8,12},{9,13},{10,... | collective-permute-start | bytes 393224 | tf_op jit(solution)/shard_map/ppermute | solution.py:394
  51.2 1.9 %collective-permute-start.3 = (bf16[32,2048]{1,0:T(8,128)(2,1)S(1)}, bf16[32,2048]{1,0:T(8,128)(2,1)S(1)}, u32[]{:S(2)}, u32[]{:S(2)}) collective-permute-start(bf16[32,2048]{1,0:T(8,128)(2,1)S(1)} %get-tuple-element.40), channel_id=1, source_target_pairs={{0,6},{1,7},{2,0},{3,1},{4,2},{5,3},{6,4},{7,5},{8,14},{9,15},{10,... | collective-permute-start | bytes 393224 | tf_op jit(solution)/shard_map/ppermute | solution.py:394
  53.2 0.0 collective-permute-done.1.refs_1_
  53.2 2.1 %collective-permute-done.2.refs_2_ = bf16[32,2048]{1,0:T(8,128)(2,1)S(1)} collective-permute-done((bf16[32,2048]{1,0:T(8,128)(2,1)S(1)}, bf16[32,2048]{1,0:T(8,128)(2,1)S(1)}, u32[]{:S(2)}, u32[]{:S(2)}) %collective-permute-start.2) | collective-permute-done | bytes 131104 | tf_op jit(solution)/shard_map/ppermute | solution.py:394
  55.3 2.4 %collective-permute-done.3.refs_3_ = bf16[32,2048]{1,0:T(8,128)(2,1)S(1)} collective-permute-done((bf16[32,2048]{1,0:T(8,128)(2,1)S(1)}, bf16[32,2048]{1,0:T(8,128)(2,1)S(1)}, u32[]{:S(2)}, u32[]{:S(2)}) %collective-permute-start.3) | collective-permute-done | bytes 131104 | tf_op jit(solution)/shard_map/ppermute | solution.py:394
  57.7 5.2 %all-to-all-done.1 = f32[32,1,2176]{2,1,0:T(1,128)S(1)} async-done(((f32[32,1,2176]{2,1,0:T(1,128)}), f32[32,1,2176]{2,1,0:T(1,128)S(1)}, u32[]{:S(2)}, u32[]{:S(2)}) %all-to-all-start.1) | async-done | bytes 278560 | tf_op jit(solution)/shard_map/all_to_all | solution.py:409
  62.8 0.7 scan.1
  63.6 9.4 %all-to-all-start.2 = ((f32[32,16,128]{2,1,0:T(8,128)}), f32[32,16,128]{2,1,0:T(8,128)S(1)}, u32[]{:S(2)}, u32[]{:S(2)}) async-start(f32[32,16,128]{2,1,0:T(8,128)} %scan.1), calls=%async_computation.2 | async-start | bytes 524288 | tf_op jit(solution)/shard_map/all_to_all | solution.py:453
  73.0 3.6 %collective-permute-start.4 = (bf16[4,32,512]{2,1,0:T(8,128)(2,1)S(1)}, bf16[4,32,512]{2,1,0:T(8,128)(2,1)S(1)}, u32[]{:S(2)}, u32[]{:S(2)}) collective-permute-start(bf16[4,32,512]{2,1,0:T(8,128)(2,1)S(1)} %get-tuple-element.48), channel_id=1, source_target_pairs={{0,1},{1,0},{2,3},{3,2},{4,5},{5,4},{6,7},{7,6},{8,9},{9,8},{10,11... | collective-permute-start | bytes 393224 | tf_op jit(solution)/shard_map/ppermute | solution.py:426
  76.6 2.2 %collective-permute-start.5 = (bf16[4,32,512]{2,1,0:T(8,128)(2,1)S(1)}, bf16[4,32,512]{2,1,0:T(8,128)(2,1)S(1)}, u32[]{:S(2)}, u32[]{:S(2)}) collective-permute-start(bf16[4,32,512]{2,1,0:T(8,128)(2,1)S(1)} %get-tuple-element.53), channel_id=1, source_target_pairs={{0,8},{1,9},{2,10},{3,11},{4,12},{5,13},{6,14},{7,15},{8,0},{9,1},... | collective-permute-start | bytes 393224 | tf_op jit(solution)/shard_map/ppermute | solution.py:426
  78.8 3.3 %collective-permute-start.6 = (bf16[4,32,512]{2,1,0:T(8,128)(2,1)S(1)}, bf16[4,32,512]{2,1,0:T(8,128)(2,1)S(1)}, u32[]{:S(2)}, u32[]{:S(2)}) collective-permute-start(bf16[4,32,512]{2,1,0:T(8,128)(2,1)S(1)} %get-tuple-element.54), channel_id=1, source_target_pairs={{0,9},{1,8},{2,11},{3,10},{4,13},{5,12},{6,15},{7,14},{8,1},{9,0},... | collective-permute-start | bytes 393224 | tf_op jit(solution)/shard_map/ppermute | solution.py:426
  82.1 0.0 collective-permute-done.4.refs_1_
  82.1 1.8 %near.1 = (f32[4,256,128]{2,1,0:T(8,128)S(1)}, bf16[4,256,256]{2,1,0:T(8,128)(2,1)S(1)}) custom-call(bf16[4,32,512]{2,1,0:T(8,128)(2,1)S(1)} %get-tuple-element.47.refs_0_, bf16[4,32,512]{2,1,0:T(8,128)(2,1)S(1)} %collective-permute-done.4.refs_1_, bf16[16,2,32,512]{3,2,1,0:T(8,128)(2,1)S(1)} %all-to-all-done.part_ref.refs_2_, ...), custom_call_target="tpu_custom_call" | custom-call | flops 250000000 | bytes 3000000 | tf_op jit(solution)/shard_map/near/pallas_call | solution.py:439
  83.9 4.1 %collective-permute-done.5.refs_0_ = bf16[4,32,512]{2,1,0:T(8,128)(2,1)S(1)} collective-permute-done((bf16[4,32,512]{2,1,0:T(8,128)(2,1)S(1)}, bf16[4,32,512]{2,1,0:T(8,128)(2,1)S(1)}, u32[]{:S(2)}, u32[]{:S(2)}) %collective-permute-start.5) | collective-permute-done | bytes 131104 | tf_op jit(solution)/shard_map/ppermute | solution.py:426
  88.0 3.8 %collective-permute-done.6.refs_1_ = bf16[4,32,512]{2,1,0:T(8,128)(2,1)S(1)} collective-permute-done((bf16[4,32,512]{2,1,0:T(8,128)(2,1)S(1)}, bf16[4,32,512]{2,1,0:T(8,128)(2,1)S(1)}, u32[]{:S(2)}, u32[]{:S(2)}) %collective-permute-start.6) | collective-permute-done | bytes 131104 | tf_op jit(solution)/shard_map/ppermute | solution.py:426
  91.8 1.8 %rest.1 = (f32[4,256,128]{2,1,0:T(8,128)S(1)}, bf16[4,256,256]{2,1,0:T(8,128)(2,1)S(1)}) custom-call(bf16[4,32,512]{2,1,0:T(8,128)(2,1)S(1)} %collective-permute-done.5.refs_0_, bf16[4,32,512]{2,1,0:T(8,128)(2,1)S(1)} %collective-permute-done.6.refs_1_, bf16[16,2,32,512]{3,2,1,0:T(8,128)(2,1)S(1)} %all-to-all-done.part_ref.refs_2_, ...), custom_call_target="tpu_custom_call" | custom-call | flops 250000000 | bytes 3000000 | tf_op jit(solution)/shard_map/rest/pallas_call | solution.py:439
  93.6 0.0 all-to-all-done.2
  93.6 0.8 close.1
  94.5 15.5 %all_to_all.20.in_ref = bf16[16,32,512]{2,1,0:T(8,128)(2,1)S(1)} all-to-all(bf16[16,32,512]{2,1,0:T(8,128)(2,1)S(1)} %close.1), channel_id=1, replica_groups={{0,1,2,3,4,5,6,7,8,9,10,11,12,13,14,15},{16,17,18,19,20,21,22,23,24,25,..., dimensions={0} | all-to-all | bytes 1048576 | tf_op jit(solution)/shard_map/all_to_all | solution.py:464
  110.0 0.8 unpack.1
  (1 shorter events, 0.0 us)
Async XLA Ops:
  2.2 10.5 %copy-start.1 = (f32[8,256]{1,0:T(8,128)S(1)}, f32[8,256]{1,0:T(8,128)}, u32[]{:S(2)}) copy-start(f32[8,256]{1,0:T(8,128)} %own_ref.1) | copy-start | bytes 24580
  2.2 13.8 %copy-start = (bf16[32,8192]{1,0:T(8,128)(2,1)S(1)}, bf16[32,8192]{1,0:T(8,128)(2,1)}, u32[]{:S(2)}) copy-start(bf16[32,8192]{1,0:T(8,128)(2,1)} %q_ref.1) | copy-start | bytes 1572868
  2.2 26.4 %all-to-all-start = ((bf16[16,2,32,512]{3,2,1,0:T(8,128)(2,1)}), bf16[16,2,32,512]{3,2,1,0:T(8,128)(2,1)S(1)}, u32[]{:S(2)}, u32[]{:S(2)}) async-start(bf16[16,2,32,512]{3,2,1,0:T(8,128)(2,1)} %pack.1), calls=%async_computation | async-start | bytes 2097152 | tf_op jit(solution)/shard_map/all_to_all | solution.py:362
  12.6 13.6 %collective-permute-start = (f32[8,256]{1,0:T(8,128)S(1)}, f32[8,256]{1,0:T(8,128)S(1)}, u32[]{:S(2)}, u32[]{:S(2)}) collective-permute-start(f32[8,256]{1,0:T(8,128)S(1)} %copy-done.1), channel_id=1, source_target_pairs={{0,8},{8,0},{16,24},{24,16},{32,40},{40,32},{48,56},{56,48},{64,72... | collective-permute-start | bytes 24584 | tf_op jit(solution)/shard_map/ppermute | solution.py:347
  16.0 12.5 %copy-start.2 = (f32[1024]{0:T(1024)S(1)}, f32[1024]{0:T(1024)}, u32[]{:S(2)}) copy-start(f32[1024]{0:T(1024)} %param.11) | copy-start | bytes 12292
  28.5 0.7 copy-start.3
  30.7 32.2 %all-to-all-start.1 = ((f32[32,1,2176]{2,1,0:T(1,128)}), f32[32,1,2176]{2,1,0:T(1,128)S(1)}, u32[]{:S(2)}, u32[]{:S(2)}) async-start(f32[32,1,2176]{2,1,0:T(1,128)} %bitcast.2), calls=%async_computation.1 | async-start | bytes 557056 | tf_op jit(solution)/shard_map/all_to_all | solution.py:409
  44.4 8.8 %collective-permute-start.1 = (bf16[32,2048]{1,0:T(8,128)(2,1)S(1)}, bf16[32,2048]{1,0:T(8,128)(2,1)S(1)}, u32[]{:S(2)}, u32[]{:S(2)}) collective-permute-start(bf16[32,2048]{1,0:T(8,128)(2,1)S(1)} %get-tuple-element.38), channel_id=1, source_target_pairs={{0,2},{1,3},{2,4},{3,5},{4,6},{5,7},{6,0},{7,1},{8,10},{9,11},{10,... | collective-permute-start | bytes 393224 | tf_op jit(solution)/shard_map/ppermute | solution.py:394
  46.3 9.0 %collective-permute-start.2 = (bf16[32,2048]{1,0:T(8,128)(2,1)S(1)}, bf16[32,2048]{1,0:T(8,128)(2,1)S(1)}, u32[]{:S(2)}, u32[]{:S(2)}) collective-permute-start(bf16[32,2048]{1,0:T(8,128)(2,1)S(1)} %get-tuple-element.39), channel_id=1, source_target_pairs={{0,4},{1,5},{2,6},{3,7},{4,0},{5,1},{6,2},{7,3},{8,12},{9,13},{10,... | collective-permute-start | bytes 393224 | tf_op jit(solution)/shard_map/ppermute | solution.py:394
  51.2 6.4 %collective-permute-start.3 = (bf16[32,2048]{1,0:T(8,128)(2,1)S(1)}, bf16[32,2048]{1,0:T(8,128)(2,1)S(1)}, u32[]{:S(2)}, u32[]{:S(2)}) collective-permute-start(bf16[32,2048]{1,0:T(8,128)(2,1)S(1)} %get-tuple-element.40), channel_id=1, source_target_pairs={{0,6},{1,7},{2,0},{3,1},{4,2},{5,3},{6,4},{7,5},{8,14},{9,15},{10,... | collective-permute-start | bytes 393224 | tf_op jit(solution)/shard_map/ppermute | solution.py:394
  63.6 30.0 %all-to-all-start.2 = ((f32[32,16,128]{2,1,0:T(8,128)}), f32[32,16,128]{2,1,0:T(8,128)S(1)}, u32[]{:S(2)}, u32[]{:S(2)}) async-start(f32[32,16,128]{2,1,0:T(8,128)} %scan.1), calls=%async_computation.2 | async-start | bytes 524288 | tf_op jit(solution)/shard_map/all_to_all | solution.py:453
  73.0 9.1 %collective-permute-start.4 = (bf16[4,32,512]{2,1,0:T(8,128)(2,1)S(1)}, bf16[4,32,512]{2,1,0:T(8,128)(2,1)S(1)}, u32[]{:S(2)}, u32[]{:S(2)}) collective-permute-start(bf16[4,32,512]{2,1,0:T(8,128)(2,1)S(1)} %get-tuple-element.48), channel_id=1, source_target_pairs={{0,1},{1,0},{2,3},{3,2},{4,5},{5,4},{6,7},{7,6},{8,9},{9,8},{10,11... | collective-permute-start | bytes 393224 | tf_op jit(solution)/shard_map/ppermute | solution.py:426
  76.6 11.4 %collective-permute-start.5 = (bf16[4,32,512]{2,1,0:T(8,128)(2,1)S(1)}, bf16[4,32,512]{2,1,0:T(8,128)(2,1)S(1)}, u32[]{:S(2)}, u32[]{:S(2)}) collective-permute-start(bf16[4,32,512]{2,1,0:T(8,128)(2,1)S(1)} %get-tuple-element.53), channel_id=1, source_target_pairs={{0,8},{1,9},{2,10},{3,11},{4,12},{5,13},{6,14},{7,15},{8,0},{9,1},... | collective-permute-start | bytes 393224 | tf_op jit(solution)/shard_map/ppermute | solution.py:426
  78.8 13.0 %collective-permute-start.6 = (bf16[4,32,512]{2,1,0:T(8,128)(2,1)S(1)}, bf16[4,32,512]{2,1,0:T(8,128)(2,1)S(1)}, u32[]{:S(2)}, u32[]{:S(2)}) collective-permute-start(bf16[4,32,512]{2,1,0:T(8,128)(2,1)S(1)} %get-tuple-element.54), channel_id=1, source_target_pairs={{0,9},{1,8},{2,11},{3,10},{4,13},{5,12},{6,15},{7,14},{8,1},{9,0},... | collective-permute-start | bytes 393224 | tf_op jit(solution)/shard_map/ppermute | solution.py:426
